TPU v7x, 256 devices: a whole 4x4x8 slice. The times are simulated.
256 devices in a mesh: section: 8 (over z_lo, core), vocab: 32 (over y, z_hi, x).
Axes of the slice: x: 4, y: 4, z: 8 (z_hi: 2, z_lo: 4; z = z_hi * 4 + z_lo), core: 2. Of those that a mesh axis runs over, the one named last changes fastest.
Arguments:
- hidden: bfloat16 [8, 512, 8192], P('section', None, 'vocab'), may hold values from -160 to 160
- final_hidden: bfloat16 [512, 8192], P('section', 'vocab'), may hold values from -160 to 160
- row_pick: int32 [8, 128], P('section'), may hold values from 0 to 511
- trans_weight: bfloat16 [8, 8192, 8192], P('section', None, 'vocab'), may hold values from -0.0625 to 0.0625
- trans_bias: bfloat16 [8, 8192], P('section', 'vocab'), may hold values from -6 to 6
- norm_gain: bfloat16 [8192], P('vocab'), may hold values from 0.5 to 1.5
- unembed: bfloat16 [8192, 16384], P('section', 'vocab'), may hold values from -100 to 100
Outputs:
- grad_weight: bfloat16 [8, 8192, 8192], P('section', None, 'vocab')
- grad_bias: float32 [8, 8192], P('section', 'vocab')
- kl_mean: float32 [8], P('section')
All inputs are finite; a program needn't handle non-finite values.
Results may differ from a plain program's by a relative error of at most 0.024.
Values may be sent and summed in bfloat16 or wider, within the bound.
A program may use at most 64 MiB of HBM per device.

v0:
```python
import jax
import jax.numpy as jnp
from jax import lax
from jax.sharding import PartitionSpec as P

epsilon = 1e-05


def combined_all(value, axis, join):
    pieces = jax.tree.map(lambda part: lax.all_gather(part, axis), value)
    head = jax.tree.map(lambda part: part[0], pieces)
    tail = jax.tree.map(lambda part: part[1:], pieces)
    so_far, _ = lax.scan(lambda so_far, section: (join(so_far, section), None), head, tail)
    return so_far


def combine_totals(first, second):
    trans_max = jnp.maximum(first[0], second[0])
    trans_sum = first[1] * jnp.exp(first[0] - trans_max) + second[1] * jnp.exp(
        second[0] - trans_max
    )
    target_max = jnp.maximum(first[2], second[2])
    target_sum = first[3] * jnp.exp(first[2] - target_max) + second[3] * jnp.exp(
        second[2] - target_max
    )
    return (trans_max, trans_sum, target_max, target_sum)


def local_totals(logits):
    highest = jnp.max(logits, axis=-1)
    return (highest, jnp.sum(jnp.exp(logits - highest[:, None]), axis=-1))


def per_device(hidden, final_hidden, row_pick, trans_weight, trans_bias, norm_gain, unembed):
    gain_cols = norm_gain.astype(jnp.float32)
    width = trans_weight.shape[1]
    row_count = row_pick.shape[1]
    unembed_full = lax.all_gather(unembed, "section", axis=0, tiled=True)
    final_cols = lax.all_gather(final_hidden, "section", axis=0, tiled=True)
    picked = row_pick[0]
    input_cols = hidden[0][picked]
    inputs = lax.all_gather(input_cols, "vocab", axis=1, tiled=True)
    trans = (
        input_cols.astype(jnp.float32)
        + jnp.dot(inputs, trans_weight[0], preferred_element_type=jnp.float32)
        + trans_bias[0].astype(jnp.float32)
    )
    finals = final_cols[picked].astype(jnp.float32)
    trans_total, final_total = lax.psum(
        (jnp.sum(trans * trans, axis=-1), jnp.sum(finals * finals, axis=-1)), "vocab"
    )
    trans_scale = lax.rsqrt(trans_total / width + epsilon)
    final_scale = lax.rsqrt(final_total / width + epsilon)
    normed = (trans * trans_scale[:, None] * gain_cols).astype(jnp.bfloat16)
    target = (finals * final_scale[:, None] * gain_cols).astype(jnp.bfloat16)
    slab_rows = unembed_full
    logits = jnp.dot(
        lax.all_gather(normed, "vocab", axis=1, tiled=True),
        slab_rows,
        preferred_element_type=jnp.float32,
    )
    target_logits = jnp.dot(
        lax.all_gather(target, "vocab", axis=1, tiled=True),
        slab_rows,
        preferred_element_type=jnp.float32,
    )
    trans_max, trans_sum = local_totals(logits)
    target_max, target_sum = local_totals(target_logits)
    totals = combined_all((trans_max, trans_sum, target_max, target_sum), "vocab", combine_totals)
    log_trans = logits - (totals[0] + jnp.log(totals[1]))[:, None]
    log_target = target_logits - (totals[2] + jnp.log(totals[3]))[:, None]
    probs = jnp.exp(log_target)
    kl_part = jnp.sum(probs * (log_target - log_trans), axis=-1)
    dlogits = (jnp.exp(log_trans) - probs).astype(jnp.bfloat16)
    kl_rows = lax.psum(kl_part, "vocab")
    slab_rows = unembed_full
    dnormed_cols = lax.psum_scatter(
        lax.dot_general(
            slab_rows, dlogits, (((1,), (1,)), ((), ())), preferred_element_type=jnp.float32
        ).astype(jnp.bfloat16),
        "vocab",
        scatter_dimension=0,
        tiled=True,
    ).astype(jnp.float32)
    trans_cols = trans.T
    scaled_cols = dnormed_cols * gain_cols[:, None]
    product = lax.psum(jnp.sum(scaled_cols * trans_cols, axis=0), "vocab") / width
    dtrans_cols = trans_scale[None, :] * (
        scaled_cols - trans_cols * (trans_scale * trans_scale * product)[None, :]
    )
    grad_weights = [
        lax.dot_general(
            inputs,
            dtrans_cols.astype(jnp.bfloat16),
            (((0,), (1,)), ((), ())),
            preferred_element_type=jnp.float32,
        ).astype(jnp.bfloat16)
    ]
    grad_biases = [jnp.sum(dtrans_cols, axis=1)]
    kl_values = [jnp.sum(kl_rows) / row_count]
    return (jnp.stack(grad_weights), jnp.stack(grad_biases), jnp.stack(kl_values))


def solution(mesh):
    placed = (
        P("section", None, "vocab"),
        P("section", "vocab"),
        P("section", None),
        P("section", None, "vocab"),
        P("section", "vocab"),
        P("vocab"),
        P("section", "vocab"),
    )
    return jax.shard_map(
        per_device,
        mesh=mesh,
        in_specs=placed,
        out_specs=(P("section", None, "vocab"), P("section", "vocab"), P("section")),
        check_vma=False,
    )
```

profile of v0, /device:TPU:2, one launch (start us, length us, event | category | flops | bytes accessed | tf_op | source)
XLA Modules:
  0.0 1215.9 jit_solution(14653384392186049527)
XLA Ops:
  7.2 0.7 fusion.34
  7.9 0.2 copy-done
  8.1 1.5 gather_fusion
  9.7 0.7 add.75
  10.4 0.7 convert_element_type.38
  11.0 15.4 %all_gather.46 = bf16[512,256]{1,0:T(8,128)(2,1)S(1)} all-gather(bf16[64,256]{1,0:T(8,128)(2,1)} %param.10), channel_id=1, replica_groups=mesh['section'=8,'vocab'=32] {'section'}, dimensions={0}, use_global_device_ids=true | all-gather | bytes 294912 | tf_op jit(solution)/shard_map/all_gather | solution.py:39
  26.4 0.8 gather_fusion.1
  27.3 84.5 %all-gather.20.cloned.1.call-done = bf16[128,8192]{1,0:T(8,128)(2,1)} async-done(((bf16[128,256]{1,0:T(8,128)(2,1)}), bf16[128,8192]{1,0:T(8,128)(2,1)}) %all-gather.20.cloned.1.call-update) | async-done | bytes 2097168 | tf_op jit(solution)/shard_map/all_gather | solution.py:42
  111.8 3.7 multiply_reduce_fusion.1
  115.4 109.8 %all-reduce.1 = (f32[128]{0:T(128)S(1)}, f32[128]{0:T(128)S(1)}) all-reduce(f32[128]{0:T(128)S(1)} %fusion.20, f32[128]{0:T(128)S(1)} %get-tuple-element.87), channel_id=1, replica_groups=mesh['section'=8,'vocab'=32] {'vocab'}, use_global_device_ids=true, to_apply=%region_5.0 | all-reduce | flops 256 | bytes 2048 | tf_op jit(solution)/shard_map/psum | solution.py:49
  225.3 0.8 multiply_convert_fusion
  226.1 0.7 all-gather.16.cloned.1.call-update
  226.9 0.5 all-gather.18.cloned.1.call-update
  227.4 90.7 %all-gather.14.cloned.1.call-done = bf16[128,8192]{1,0:T(8,128)(2,1)} async-done(((bf16[128,256]{1,0:T(8,128)(2,1)}), bf16[128,8192]{1,0:T(8,128)(2,1)}) %all-gather.14.cloned.1.call-update) | async-done | bytes 2097168 | tf_op jit(solution)/shard_map/all_gather | solution.py:58
  318.2 91.2 %all-gather.16.cloned.1.call-done = bf16[8192,512]{1,0:T(8,128)(2,1)} async-done(((bf16[1024,512]{1,0:T(8,128)(2,1)}), bf16[8192,512]{1,0:T(8,128)(2,1)}) %all-gather.16.cloned.1.call-update) | async-done | bytes 8388624 | tf_op jit(solution)/shard_map/all_gather | solution.py:38
  409.4 5.4 fusion.37
  414.8 107.7 %all-gather.5 = f32[32,1,128]{2,1,0:T(1,128)S(1)} all-gather(f32[1,1,128]{2,1,0:T(1,128)S(1)} %bitcast.100), channel_id=3, replica_groups=mesh['section'=8,'vocab'=32] {'vocab'}, dimensions={0}, use_global_device_ids=true | all-gather | bytes 16896 | tf_op jit(solution)/shard_map/all_gather | solution.py:10
  522.5 0.2 exponential_reduce_fusion.1
  522.6 115.5 %all-gather.6 = f32[32,1,128]{2,1,0:T(1,128)S(1)} all-gather(f32[1,1,128]{2,1,0:T(1,128)S(1)} %bitcast.102), channel_id=4, replica_groups=mesh['section'=8,'vocab'=32] {'vocab'}, dimensions={0}, use_global_device_ids=true | all-gather | bytes 16896 | tf_op jit(solution)/shard_map/all_gather | solution.py:10
  638.2 5.4 fusion.38
  643.6 106.6 %all-gather.7 = f32[32,1,128]{2,1,0:T(1,128)S(1)} all-gather(f32[1,1,128]{2,1,0:T(1,128)S(1)} %bitcast.99), channel_id=5, replica_groups=mesh['section'=8,'vocab'=32] {'vocab'}, dimensions={0}, use_global_device_ids=true | all-gather | bytes 16896 | tf_op jit(solution)/shard_map/all_gather | solution.py:10
  750.1 0.2 exponential_reduce_fusion
  750.3 108.6 %all-gather.8 = f32[32,1,128]{2,1,0:T(1,128)S(1)} all-gather(f32[1,1,128]{2,1,0:T(1,128)S(1)} %bitcast.103), channel_id=6, replica_groups=mesh['section'=8,'vocab'=32] {'vocab'}, dimensions={0}, use_global_device_ids=true | all-gather | bytes 16896 | tf_op jit(solution)/shard_map/all_gather | solution.py:10
  858.9 1.5 while.16
  860.5 7.5 fusion.11
  868.0 0.2 multiply_reduce_fusion
  868.3 214.5 %reduce-scatter.2.cloned.1.call-done = bf16[256,128]{0,1:T(8,128)(2,1)} async-done(((bf16[8192,128]{0,1:T(8,128)(2,1)}), bf16[256,128]{0,1:T(8,128)(2,1)}) %reduce-scatter.2.cloned.1.call-update) | async-done | bytes 65552 | tf_op jit(solution)/shard_map/reduce_scatter | solution.py:77
  1082.8 1.0 fusion.23
  1083.8 118.2 %all-reduce = (f32[128]{0:T(128)S(1)}, f32[128]{0:T(128)S(1)}) all-reduce(f32[128]{0:T(128)S(1)} %fusion.23, f32[128]{0:T(128)S(1)} %multiply_reduce_fusion), channel_id=1, replica_groups=mesh['section'=8,'vocab'=32] {'vocab'}, use_global_device_ids=true, to_apply=%region_12.13 | all-reduce | flops 256 | bytes 2048 | tf_op jit(solution)/shard_map/psum | solution.py:87
  1202.1 0.6 reduce_sum.79
  1203.4 4.2 fusion.10
  1207.5 0.7 fusion.28
  (63 shorter events, 1.5 us)
Async XLA Ops:
  7.2 1.0 copy-start
  7.2 104.6 %all-gather.20.cloned.1.call-start = ((), (), s32[]{:S(2)}) async-start(), calls=%async_computation.5 | async-start | bytes 2162688 | tf_op jit(solution)/shard_map/all_gather | solution.py:42
  9.6 308.6 %all-gather.14.cloned.1.call-start = ((), (), s32[]{:S(2)}) async-start(), calls=%async_computation.1 | async-start | bytes 2162688 | tf_op jit(solution)/shard_map/all_gather | solution.py:58
  226.1 183.3 %all-gather.16.cloned.1.call-start = ((), (), s32[]{:S(2)}) async-start(), calls=%async_computation.2 | async-start | bytes 9437184 | tf_op jit(solution)/shard_map/all_gather | solution.py:38
  226.8 411.4 %all-gather.18.cloned.1.call-start = ((), (), s32[]{:S(2)}) async-start(), calls=%async_computation.3 | async-start | bytes 2162688 | tf_op jit(solution)/shard_map/all_gather | solution.py:63
  227.4 855.4 %reduce-scatter.2.cloned.1.call-start = ((), (), s32[]{:S(2)}) async-start(), calls=%async_computation.4 | async-start | bytes 2162688 | tf_op jit(solution)/shard_map/reduce_scatter | solution.py:77
  868.0 335.3 %copy-start.1 = (bf16[128,8192]{1,0:T(8,128)(2,1)S(1)}, bf16[128,8192]{1,0:T(8,128)(2,1)}, u32[]{:S(2)}) copy-start(bf16[128,8192]{1,0:T(8,128)(2,1)} %all-gather.20.cloned.1.call-done) | copy-start | bytes 6291460
  1082.8 124.7 %copy-start.2 = (bf16[256,128]{0,1:T(8,128)(2,1)S(1)}, bf16[256,128]{0,1:T(8,128)(2,1)}, u32[]{:S(2)}) copy-start(bf16[256,128]{0,1:T(8,128)(2,1)} %reduce-scatter.2.cloned.1.call-done) | copy-start | bytes 196612
Sparse Core Ops, SparseCore 0:
  11.8 99.9 all-gather.19
  226.2 91.9 all-gather.13
  320.0 89.4 all-gather.15
  412.5 95.5 all-gather.17
  868.2 214.5 reduce-scatter.1
where the time goes:
time: 1220 us
  blocking collectives  682 us (56%)
  waiting for transfers between devices  482 us (40%)
  matrix products  26.1 us (2%)
  between operations  15.7 us (1%)
    all_gather x4, blocking collectives, combined_all(): pieces = jax.tree.map(lambda part: lax.all_gather(part, axis), value)  438 us
    reduce_scatter x1, waiting for transfers between devices, per_device(): lax.psum_scatter(lax.dot_general(slab_rows, dlogits, (((1,), (1,)), ((),...  215 us
    psum x1, blocking collectives, per_device(): lax.psum(jnp.sum(scaled_cols * trans_cols, axis=0), 'vocab') / width  118 us
    psum x1, blocking collectives, per_device(): lax.psum((jnp.sum(trans * trans, axis=-1), jnp.sum(finals * finals, axis=...  110 us
    all_gather x1, waiting for transfers between devices, per_device(): unembed_full = lax.all_gather(unembed, 'section', axis=0, tiled=True)  91.2 us
    all_gather x1, waiting for transfers between devices, per_device(): lax.all_gather(normed, 'vocab', axis=1, tiled=True)  90.7 us
    all_gather x1, waiting for transfers between devices, per_device(): inputs = lax.all_gather(input_cols, 'vocab', axis=1, tiled=True)  84.5 us
  transfers between devices with their start and end apart: 5, of which 4 were waited for; matrix products, arithmetic and copies ran while one was open for 1% of the time, Pallas kernels for 0%

commit v1 on v0

v1 whole, which is shorter than its diff:
```python
import jax
import jax.numpy as jnp
from jax import lax
from jax.experimental import pallas as pl
from jax.experimental.pallas import tpu as pltpu
from jax.sharding import PartitionSpec as P

MESH = pl.DeviceIdType.MESH
F32, BF16 = jnp.float32, jnp.bfloat16
EPS = 1e-05
NV, NS = 32, 8
ROWS, POOL, D, VOC, FB = 128, 512, 8192, 512, 256
VMEM_LIMIT = 60 * 1024 * 1024
N_MSG = 40


def vid(y, x, zh):
    return y * 8 + zh * 4 + x


def ring(a, c):
    return lax.rem(a + (c + 4), 4)


class Place:
    def __init__(self):
        self.v = lax.axis_index("vocab")
        self.s = lax.axis_index("section")
        self.x = lax.rem(self.v, 4)
        self.zh = lax.rem(self.v // 4, 2)
        self.y = self.v // 8
        self.own = self.y * 4 + self.x

    def to(self, v):
        return (self.s, v)

    def partner(self):
        return self.to(vid(self.y, self.x, 1 - self.zh))

    def near(self, half, stage, step):
        along_x = (half == 0) == (stage == 1)
        if along_x:
            return self.to(vid(self.y, ring(self.x, step), self.zh))
        return self.to(vid(ring(self.y, step), self.x, self.zh))

    def pair(self, half, c, d):
        if half == 0:
            return ring(self.y, d) * 4 + ring(self.x, c)
        return ring(self.y, c) * 4 + ring(self.x, d)


def remote(src, dst, send_sem, recv_sem, device):
    return pltpu.make_async_remote_copy(
        src_ref=src, dst_ref=dst, send_sem=send_sem, recv_sem=recv_sem, device_id=device, device_id_type=MESH
    )


def greet(place, sections):
    barrier = pltpu.get_barrier_semaphore()

    @pl.loop(1, NV)
    def _(k):
        pl.semaphore_signal(
            barrier, inc=1, device_id=place.to(lax.rem(place.v + k, NV)), device_id_type=MESH
        )

    if sections:

        @pl.loop(1, NS)
        def _(k):
            pl.semaphore_signal(
                barrier, inc=1, device_id=(lax.rem(place.s + k, NS), place.v), device_id_type=MESH
            )

    pl.semaphore_wait(barrier, NV - 1 + (NS - 1 if sections else 0))


def send_stats(place, stats, send_sem, recv_sem):
    @pl.loop(1, NV)
    def _(k):
        remote(
            stats.at[place.v],
            stats.at[place.v],
            send_sem.at[k],
            recv_sem.at[place.v],
            place.to(lax.rem(place.v + k, NV)),
        ).start()


def wait_stats(place, stats, send_sem, recv_sem):
    @pl.loop(1, NV)
    def _(k):
        src = lax.rem(place.v + k, NV)
        copy = remote(stats.at[src], stats.at[src], send_sem.at[k], recv_sem.at[src], place.to(src))
        copy.wait_send()
        copy.wait_recv()


def to_lanes(columns):
    lane = lax.broadcasted_iota(jnp.int32, (ROWS, 128), 1)
    tile = jnp.zeros((ROWS, 128), F32)
    for k, column in enumerate(columns):
        tile = jnp.where(lane == k, column, tile)
    return tile.T[0:8, :]


def to_columns(tile):
    return jnp.concatenate([tile, jnp.zeros((120, 128), F32)], axis=0).T


class Gather:
    ORDER = (0, -1, 1, 2)

    def __init__(self, place, buf, send_sem, recv_sem):
        self.place, self.buf, self.ss, self.rs = place, buf, send_sem, recv_sem
        self.rows = buf.shape[2]
        self.sent = []
        self.ids = {}

    def span(self, half, part):
        h, q = self.rows // 2, self.rows // 4
        if part == "all":
            return pl.ds(half * h, h)
        return pl.ds(half * h + (0 if part == "first" else q), q)

    def key(self, *name):
        return self.ids.setdefault(name, len(self.ids))

    def move(self, name, pair, half, part, device):
        ref = self.buf.at[pair, :, self.span(half, part), :]
        k = self.key(*name)
        return remote(ref, ref, self.ss.at[k], self.rs.at[k], device)

    def send(self, half, stage, col, c, d, part, step):
        p = self.place
        copy = self.move((half, stage, col, part, step), p.pair(half, c, d), half, part, p.near(half, stage, step))
        copy.start()
        self.sent.append(copy)

    def wait(self, half, stage, col, c, d, part, step):
        p = self.place
        self.move((half, stage, col, part, step), p.pair(half, c, d), half, part, p.near(half, stage, -step)).wait_recv()

    def partner(self, zsend, zrecv):
        p = self.place
        mine = self.buf.at[p.own, p.zh]
        return (
            remote(mine, mine, zsend, zrecv, p.partner()),
            remote(self.buf.at[p.own, 1 - p.zh], self.buf.at[p.own, 1 - p.zh], zsend, zrecv, p.partner()),
        )

    def run(self, zsend, zrecv):
        out, back = self.partner(zsend, zrecv)
        out.start()
        back.wait_recv()
        for half in (0, 1):
            for step in (1, -1):
                self.send(half, 1, 0, 0, 0, "all", step)
        for half in (0, 1):
            for step in (1, -1):
                self.send(half, 2, 0, 0, 0, "all", step)
        for step, part in ((1, "first"), (-1, "second")):
            for half in (0, 1):
                self.wait(half, 1, 0, -step, 0, "all", step)
                self.send(half, 1, 0, -step, 0, part, step)
                for turn in (1, -1):
                    self.send(half, 2, -step, -step, 0, "all", turn)
        for step, part in ((1, "first"), (-1, "second")):
            for half in (0, 1):
                self.wait(half, 2, 0, 0, -step, "all", step)
                self.send(half, 2, 0, 0, -step, part, step)
        for half in (0, 1):
            self.wait(half, 1, 0, 2, 0, "first", 1)
            self.wait(half, 1, 0, 2, 0, "second", -1)
            for turn in (1, -1):
                self.send(half, 2, 2, 2, 0, "all", turn)
        for c in (-1, 1, 2):
            for step, part in ((1, "first"), (-1, "second")):
                for half in (0, 1):
                    self.wait(half, 2, c, c, -step, "all", step)
                    self.send(half, 2, c, c, -step, part, step)
        for c in self.ORDER:
            for half in (0, 1):
                self.wait(half, 2, c, c, 2, "first", 1)
                self.wait(half, 2, c, c, 2, "second", -1)
        out.wait_send()
        for copy in self.sent:
            copy.wait_send()


def kernel_a(
    pick, hidden, final, w_hbm, bias, gain, x_out, lt_out, trans_out, scale_out,
    xbuf, ltbuf, fbuf, wbuf, stats, acc, w_sem, o_sem, fs, fr, zs, zr, ss1, rs1, ss2, rs2, sts, str_,
):
    place = Place()
    w_copy = pltpu.make_async_copy(w_hbm, wbuf, w_sem)
    w_copy.start()
    onehot = jnp.where(lax.broadcasted_iota(jnp.int32, (ROWS, POOL), 1) == pick[...], 1.0, 0.0).astype(BF16)
    inputs = jnp.dot(onehot, hidden[...], preferred_element_type=F32)
    xbuf[place.own, place.zh] = inputs.astype(BF16)
    greet(place, True)

    @pl.loop(1, NS)
    def _(k):
        remote(
            final, fbuf.at[place.s], fs.at[k], fr.at[place.s], (lax.rem(place.s + k, NS), place.v)
        ).start()

    fbuf[place.s] = final[...]
    Gather(place, xbuf, ss1, rs1).run(zs.at[0], zr.at[0])
    x_copy = pltpu.make_async_copy(xbuf, x_out, o_sem.at[0])
    x_copy.start()

    @pl.loop(1, NS)
    def _(k):
        src = lax.rem(place.s + k, NS)
        copy = remote(fbuf.at[src], fbuf.at[src], fs.at[k], fr.at[src], (src, place.v))
        copy.wait_send()
        copy.wait_recv()

    finals = jnp.dot(onehot, fbuf[...].reshape(POOL, FB), preferred_element_type=F32)
    w_copy.wait()
    acc[...] = xbuf[place.own, place.zh].astype(F32) + bias[...].astype(F32)

    @pl.loop(0, 16)
    def _(p):
        y, x = p // 4, lax.rem(p, 4)
        total = acc[...]
        for zh in (0, 1):
            rows = pl.ds(pl.multiple_of(vid(y, x, zh) * FB, FB), FB)
            total = total + jnp.dot(xbuf[p, zh], wbuf[rows, :], preferred_element_type=F32)
        acc[...] = total

    trans = acc[...]
    gain_cols = gain[...].astype(F32)
    ltbuf[place.own, place.zh, 0:ROWS] = (trans * gain_cols).astype(BF16)
    ltbuf[place.own, place.zh, ROWS : 2 * ROWS] = (finals * gain_cols).astype(BF16)
    stats[place.v] = to_lanes(
        [jnp.sum(trans * trans, axis=1, keepdims=True), jnp.sum(finals * finals, axis=1, keepdims=True)]
    )
    trans_out[...] = trans
    send_stats(place, stats, sts, str_)
    Gather(place, ltbuf, ss2, rs2).run(zs.at[1], zr.at[1])
    lt_copy = pltpu.make_async_copy(ltbuf, lt_out, o_sem.at[1])
    lt_copy.start()
    wait_stats(place, stats, sts, str_)
    scale_out[...] = lax.rsqrt(jnp.sum(stats[...], axis=0) / D + EPS)
    x_copy.wait()
    lt_copy.wait()


def kernel_b(
    lt_hbm, u_hbm, trans, scale, gain, dtrans_out, bias_out, kl_out,
    lt, u, acc, stats, part, sbuf, rq, rp, rm, r1p, r1m, rz, in_sem, sts, str_, ss, rs, zs, zr,
):
    place = Place()
    chunk = D // 8
    lt_copy = pltpu.make_async_copy(lt_hbm, lt, in_sem.at[8])
    lt_copy.start()
    u_copies = []
    for i in range(8):
        rows = pl.ds(i * chunk, chunk)
        u_copies.append(pltpu.make_async_copy(u_hbm.at[rows], u.at[rows], in_sem.at[i]))
        u_copies[-1].start()
    greet(place, False)
    lt_copy.wait()
    for i in range(8):
        u_copies[i].wait()
        total = acc[...] if i > 0 else None
        for v in range(4 * i, 4 * i + 4):
            p, zh = (v // 8) * 4 + v % 4, (v // 4) % 2
            term = jnp.dot(lt[p, zh], u[v * FB : (v + 1) * FB, :], preferred_element_type=F32)
            total = term if total is None else total + term
        acc[...] = total
    columns = to_columns(scale[...])
    trans_scale, final_scale = columns[:, 0:1], columns[:, 1:2]
    logits = acc[0:ROWS] * trans_scale
    target = acc[ROWS : 2 * ROWS] * final_scale

    def totals(values):
        highest = jnp.max(values, axis=1, keepdims=True)
        shifted = values - highest
        weights = jnp.exp(shifted)
        return highest, shifted, weights, jnp.sum(weights, axis=1, keepdims=True)

    l_max, l_shift, l_exp, l_sum = totals(logits)
    t_max, t_shift, t_exp, t_sum = totals(target)
    stats[place.v] = to_lanes(
        [
            l_max,
            l_sum,
            jnp.sum(l_exp * l_shift, axis=1, keepdims=True),
            t_max,
            t_sum,
            jnp.sum(t_exp * t_shift, axis=1, keepdims=True),
            jnp.sum(t_exp * l_shift, axis=1, keepdims=True),
        ]
    )
    send_stats(place, stats, sts, str_)
    wait_stats(place, stats, sts, str_)
    lm, ls, la, tm, ts, ta, tb = (stats[:, k, :] for k in range(7))

    def over(values):
        return jnp.sum(values, axis=0, keepdims=True)

    l_top = jnp.max(lm, axis=0, keepdims=True)
    t_top = jnp.max(tm, axis=0, keepdims=True)
    lw, tw = jnp.exp(lm - l_top), jnp.exp(tm - t_top)
    l_total, t_total = over(lw * ls), over(tw * ts)
    mean_l = over(lw * (la + ls * (lm - l_top))) / l_total
    mean_t = over(tw * (ta + ts * (tm - t_top))) / t_total
    mean_tl = over(tw * (tb + ts * (lm - l_top))) / t_total
    kl_rows = mean_t - mean_tl - jnp.log(t_total) + jnp.log(l_total)
    kl_out[...] = jnp.broadcast_to(jnp.sum(kl_rows, axis=1, keepdims=True) / ROWS, (8, 128))
    l_norm = l_top + jnp.log(l_total)
    t_norm = t_top + jnp.log(t_total)
    pull = scale[0:1, :] * (mean_l - mean_tl) / D
    columns = to_columns(jnp.concatenate([l_norm, t_norm, pull, jnp.zeros((5, 128), F32)], axis=0))
    l_norm, t_norm, pull = columns[:, 0:1], columns[:, 1:2], columns[:, 2:3]
    dlogits = (jnp.exp(logits - l_norm) - jnp.exp(target - t_norm)).astype(BF16)

    ids = {}
    sent = []
    half_rows, quarter = ROWS // 2, ROWS // 4

    def span(half, name):
        if name == "all":
            return pl.ds(half * half_rows, half_rows)
        return pl.ds(half * half_rows + (0 if name == "first" else quarter), quarter)

    def product(pair):
        y, x = pair // 4, lax.rem(pair, 4)
        for zh in (0, 1):
            rows = pl.ds(pl.multiple_of(vid(y, x, zh) * FB, FB), FB)
            part[pair, zh] = lax.dot_general(
                dlogits, u[rows, :], (((1,), (1,)), ((), ())), preferred_element_type=F32
            )

    def move(name, src, dst, device):
        k = ids.setdefault(name, len(ids))
        return remote(src, dst, ss.at[k], rs.at[k], device)

    def landing(stage, name, step, pair, half):
        rows = span(half, name)
        if name != "all":
            return rq.at[pair, :, rows, :]
        if stage == 2:
            return (rp if step == 1 else rm).at[pair, :, rows, :]
        return (r1p if step == 1 else r1m).at[:, rows, :]

    def send(half, stage, col, c, d, name, step):
        pair = place.pair(half, c, d)
        copy = move(
            (half, stage, col, name, step),
            sbuf.at[pair, :, span(half, name), :],
            landing(stage, name, step, pair, half),
            place.near(half, stage, step),
        )
        copy.start()
        sent.append(copy)

    def receive(half, stage, col, c, d, name, step):
        pair = place.pair(half, c, d)
        ref = landing(stage, name, step, pair, half)
        move((half, stage, col, name, step), ref, ref, place.near(half, stage, -step)).wait_recv()
        return ref[...].astype(F32)

    def put(half, c, d, name, value):
        sbuf[place.pair(half, c, d), :, span(half, name), :] = value.astype(BF16)

    def mine(half, c, d, name):
        return part[place.pair(half, c, d), :, span(half, name), :]

    first = [(2, 2)] + [(2, k) for k in (-1, 1, 0)] + [(k, 2) for k in (-1, 1, 0)]
    later = [(-1, -1), (-1, 1), (1, -1), (1, 1), (0, -1), (0, 1), (-1, 0), (1, 0), (0, 0)]
    for dx, dy in first:
        product(place.pair(0, dx, dy))
        for half in (0, 1):
            c, d = (dx, dy) if half == 0 else (dy, dx)
            if d == 2:
                put(half, c, 2, "all", mine(half, c, 2, "all"))
                send(half, 2, c, c, 2, "first", -1)
                send(half, 2, c, c, 2, "second", 1)
    for dx, dy in later:
        product(place.pair(0, dx, dy))
    order = (2, -1, 1, 0)
    for c in order:
        for half in (0, 1):
            for step, name in ((-1, "first"), (1, "second")):
                arrived = receive(half, 2, c, c, step, name, step)
                put(half, c, step, "all", mine(half, c, step, "all"))
                put(half, c, step, name, mine(half, c, step, name) + arrived)
                send(half, 2, c, c, step, "all", step)
    own_sum = [None, None]
    for c in order:
        for half in (0, 1):
            total = mine(half, c, 0, "all")
            for step in (1, -1):
                total = total + receive(half, 2, c, c, 0, "all", step)
            if c == 2:
                put(half, 2, 0, "all", total)
                send(half, 1, 0, 2, 0, "first", -1)
                send(half, 1, 0, 2, 0, "second", 1)
            elif c != 0:
                name = "first" if c == -1 else "second"
                arrived = receive(half, 1, 0, c, 0, name, c)
                zero = jnp.zeros_like(arrived)
                pieces = [arrived, zero] if name == "first" else [zero, arrived]
                put(half, c, 0, "all", total + jnp.concatenate(pieces, axis=1))
                send(half, 1, 0, c, 0, "all", c)
            else:
                for step in (1, -1):
                    total = total + receive(half, 1, 0, 0, 0, "all", step)
                put(half, 0, 0, "all", total)
                part[place.own, :, span(half, "all"), :] = total
    out = remote(sbuf.at[place.own, 1 - place.zh], rz, zs, zr, place.partner())
    out.start()
    out.wait_recv()
    dnormed = part[place.own, place.zh] + rz[...].astype(F32)
    scaled = dnormed * gain[...].astype(F32)
    dtrans = trans_scale * (scaled - trans[...] * pull)
    dtrans_out[...] = dtrans.astype(BF16)
    bias_out[...] = jnp.sum(dtrans, axis=0, keepdims=True)
    out.wait_send()
    for copy in sent:
        copy.wait_send()


def kernel_c(x, dtrans, out):
    out[...] = lax.dot_general(
        x[0, 0], dtrans[...], (((0,), (0,)), ((), ())), preferred_element_type=F32
    ).astype(BF16)


def per_device(hidden, final_hidden, row_pick, trans_weight, trans_bias, norm_gain, unembed):
    unembed_full = lax.all_gather(unembed, "section", axis=0, tiled=True)
    whole = pl.BlockSpec(memory_space=pltpu.VMEM)
    anywhere = pl.BlockSpec(memory_space=pl.ANY)
    dma = pltpu.SemaphoreType.DMA
    gain = norm_gain.reshape(1, FB)
    shape = jax.ShapeDtypeStruct
    x_all, lt_all, trans, scale = pl.pallas_call(
        kernel_a,
        name="gather_rows",
        out_shape=(
            shape((16, 2, ROWS, FB), BF16),
            shape((16, 2, 2 * ROWS, FB), BF16),
            shape((ROWS, FB), F32),
            shape((8, 128), F32),
        ),
        in_specs=[whole, whole, whole, anywhere, whole, whole],
        out_specs=(anywhere, anywhere, whole, whole),
        scratch_shapes=[
            pltpu.VMEM((16, 2, ROWS, FB), BF16),
            pltpu.VMEM((16, 2, 2 * ROWS, FB), BF16),
            pltpu.VMEM((NS, POOL // NS, FB), BF16),
            pltpu.VMEM((D, FB), BF16),
            pltpu.VMEM((NV, 8, 128), F32),
            pltpu.VMEM((ROWS, FB), F32),
            dma,
            dma((2,)),
            dma((NS,)),
            dma((NS,)),
            dma((2,)),
            dma((2,)),
            dma((N_MSG,)),
            dma((N_MSG,)),
            dma((N_MSG,)),
            dma((N_MSG,)),
            dma((NV,)),
            dma((NV,)),
        ],
        compiler_params=pltpu.CompilerParams(
            collective_id=0, has_side_effects=True, vmem_limit_bytes=VMEM_LIMIT
        ),
        cost_estimate=pl.CostEstimate(flops=10**9, bytes_accessed=10**8, transcendentals=0),
    )(row_pick.reshape(ROWS, 1), hidden[0], final_hidden, trans_weight[0], trans_bias, gain)
    dtrans, grad_bias, kl = pl.pallas_call(
        kernel_b,
        name="softmax_scatter",
        out_shape=(shape((ROWS, FB), BF16), shape((1, FB), F32), shape((8, 128), F32)),
        in_specs=[anywhere, anywhere, whole, whole, whole],
        out_specs=(whole, whole, whole),
        scratch_shapes=[
            pltpu.VMEM((16, 2, 2 * ROWS, FB), BF16),
            pltpu.VMEM((D, VOC), BF16),
            pltpu.VMEM((2 * ROWS, VOC), F32),
            pltpu.VMEM((NV, 8, 128), F32),
            pltpu.VMEM((16, 2, ROWS, FB), F32),
            pltpu.VMEM((16, 2, ROWS, FB), BF16),
            pltpu.VMEM((16, 2, ROWS, FB), BF16),
            pltpu.VMEM((16, 2, ROWS, FB), BF16),
            pltpu.VMEM((16, 2, ROWS, FB), BF16),
            pltpu.VMEM((2, ROWS, FB), BF16),
            pltpu.VMEM((2, ROWS, FB), BF16),
            pltpu.VMEM((ROWS, FB), BF16),
            dma((9,)),
            dma((NV,)),
            dma((NV,)),
            dma((N_MSG,)),
            dma((N_MSG,)),
            dma,
            dma,
        ],
        compiler_params=pltpu.CompilerParams(
            collective_id=1, has_side_effects=True, vmem_limit_bytes=VMEM_LIMIT
        ),
        cost_estimate=pl.CostEstimate(flops=10**9, bytes_accessed=10**8, transcendentals=0),
    )(lt_all, unembed_full, trans, scale, gain)
    grad_weight = pl.pallas_call(
        kernel_c,
        name="weight_gradient",
        grid=(NV,),
        out_shape=shape((D, FB), BF16),
        in_specs=[
            pl.BlockSpec((1, 1, ROWS, FB), lambda v: ((v // 8) * 4 + v % 4, (v // 4) % 2, 0, 0)),
            pl.BlockSpec((ROWS, FB), lambda v: (0, 0)),
        ],
        out_specs=pl.BlockSpec((FB, FB), lambda v: (v, 0)),
    )(x_all, dtrans)
    return grad_weight[None], grad_bias, kl[0, 0:1]


def solution(mesh):
    placed = (
        P("section", None, "vocab"),
        P("section", "vocab"),
        P("section", None),
        P("section", None, "vocab"),
        P("section", "vocab"),
        P("vocab"),
        P("section", "vocab"),
    )
    return jax.shard_map(
        per_device,
        mesh=mesh,
        in_specs=placed,
        out_specs=(P("section", None, "vocab"), P("section", "vocab"), P("section")),
        check_vma=False,
    )
```

time: 1220 us -> 190 us (0.16)
  blocking collectives: 682 us -> 0 us
  waiting for transfers between devices: 482 us -> 21.1 us
  Pallas kernels: 0 us -> 147 us
  matrix products: 26.1 us -> 0 us
    all_gather x5 -> x0, blocking collectives: 454 us -> none  [the longest x4 438 us: combined_all(): pieces = jax.tree.map(lambda part: lax.all_gather(part, axis), value)]
    psum x2 -> x0, blocking collectives: 228 us -> none  [the longest x1 118 us: per_device(): lax.psum(jnp.sum(scaled_cols * trans_cols, axis=0), 'vocab') / width]
    reduce_scatter x1 -> x0, waiting for transfers between devices: 215 us -> none  [per_device(): lax.psum_scatter(lax.dot_general(slab_rows, dlogits, (((1,), (1,)), ((),...]
    all_gather x3 -> x0, waiting for transfers between devices: 175 us -> none  [the longest x1 90.7 us: per_device(): lax.all_gather(normed, 'vocab', axis=1, tiled=True)]
    pallas_call x0 -> x3, Pallas kernels: none -> 147 us  [the longest x1 89.2 us: per_device(): pl.pallas_call(kernel_a, name='gather_rows', out_shape=(shape((16, 2, ROW...]
    all_gather x1, waiting for transfers between devices: 91.2 us -> 20.4 us  [per_device(): unembed_full = lax.all_gather(unembed, 'section', axis=0, tiled=True)]
    dot_general x5 -> x0, matrix products: 26.1 us -> none  [the longest x1 7.53 us: per_device(): lax.dot_general(slab_rows, dlogits, (((1,), (1,)), ((), ())), preferred_e...]
  transfers between devices with their start and end apart: 5 -> 1, of which waited for: 4 -> 1; matrix products, arithmetic and copies ran while one was open for 1% -> 1% of each run, Pallas kernels for 0% -> 48%
where the time goes in v1:
time: 190 us; the launch traced here: 187 us
  Pallas kernels  147 us (77%)
  waiting for transfers between devices  21.1 us (11%)
  between operations  14.1 us (7%)
  local copies, waits for them, and re-layouts  4.36 us (2%)
    pallas_call x1, Pallas kernels, per_device(): pl.pallas_call(kernel_a, name='gather_rows', out_shape=(shape((16, 2, ROW...  89.2 us
    pallas_call x1, Pallas kernels, per_device(): pl.pallas_call(kernel_b, name='softmax_scatter', out_shape=(shape((ROWS,...  38.6 us
    all_gather x1, waiting for transfers between devices, per_device(): unembed_full = lax.all_gather(unembed, 'section', axis=0, tiled=True)  20.4 us
    pallas_call x1, Pallas kernels, per_device(): pl.pallas_call(kernel_c, name='weight_gradient', grid=(NV,), out_shape=sh...  19.4 us
  transfers between devices with their start and end apart: 1, of which 1 were waited for; matrix products, arithmetic and copies ran while one was open for 1% of the time, Pallas kernels for 48%

profile of v1, /device:TPU:2, one launch (start us, length us, event | category | flops | bytes accessed | tf_op | source)
XLA Modules:
  0.0 186.7 jit_solution(5171534388661230247)
XLA Ops:
  7.2 0.0 all-gather.2.cloned.1.call-start
  7.2 0.7 all-gather.2.cloned.1.call-update
  7.9 1.4 copy.10.pick
  9.3 1.2 reshape.13.gain
  10.5 89.2 %gather_rows.1 = (bf16[16,2,128,256]{3,2,1,0:T(8,128)(2,1)}, bf16[16,2,256,256]{3,2,1,0:T(8,128)(2,1)}, f32[128,256]{1,0:T(8,128)}, f32[8,128]{1,0:T(8,128)}) custom-call(s32[128,1]{1,0:T(8,128)} %copy.10.pick, bf16[512,256]{1,0:T(8,128)(2,1)} %bitcast.7, bf16[64,256]{1,0:T(8,128)(2,1)} %final.1, bf16[8192,256]{1,0:T(8,128)(2,1)} %bitcast.6, ...), custom_call_target="tpu_custom_call" | custom-call | flops 1000000000 | bytes 100000000 | tf_op jit(solution)/shard_map/gather_rows/pallas_call | solution.py:442
  99.8 20.4 %all-gather.2.cloned.1.call-done.u_hbm = bf16[8192,512]{1,0:T(8,128)(2,1)} async-done(((bf16[1024,512]{1,0:T(8,128)(2,1)}), bf16[8192,512]{1,0:T(8,128)(2,1)}) %all-gather.2.cloned.1.call-update) | async-done | bytes 8388624 | tf_op jit(solution)/shard_map/all_gather | solution.py:436
  120.1 38.6 %softmax_scatter.1 = (bf16[128,256]{1,0:T(8,128)(2,1)}, f32[1,256]{1,0:T(1,128)}, f32[8,128]{1,0:T(8,128)}) custom-call(bf16[16,2,256,256]{3,2,1,0:T(8,128)(2,1)} %get-tuple-element.11.lt_hbm, bf16[8192,512]{1,0:T(8,128)(2,1)} %all-gather.2.cloned.1.call-done.u_hbm, f32[128,256]{1,0:T(8,128)} %get-tuple-element.12.trans, f32[8,128]{1,0:T(8,128)} %get-tuple-element.13.scale, ...), custom_call_target="tpu_custom_call" | custom-call | flops 1000000000 | bytes 100000000 | tf_op jit(solution)/shard_map/softmax_scatter/pallas_call | solution.py:478
  158.7 0.0 copy-start
  158.7 1.2 slice.3
  159.9 19.4 %weight_gradient.1 = bf16[8192,256]{1,0:T(8,128)(2,1)} custom-call(bf16[16,2,128,256]{3,2,1,0:T(8,128)(2,1)} %get-tuple-element.10.x, bf16[128,256]{1,0:T(8,128)(2,1)} %get-tuple-element.14.dtrans), custom_call_target="tpu_custom_call" | custom-call | tf_op jit(solution)/shard_map/weight_gradient/pallas_call | solution.py:510
  179.3 0.0 copy-done
  179.3 0.6 copy.12
Async XLA Ops:
  7.2 113.0 %all-gather.2.cloned.1.call-start = ((), (), s32[]{:S(2)}) async-start(), calls=%async_computation | async-start | bytes 9437184 | tf_op jit(solution)/shard_map/all_gather | solution.py:436
  158.7 20.6 %copy-start = (f32[1,256]{1,0:T(1,128)S(1)}, f32[1,256]{1,0:T(1,128)}, u32[]{:S(2)}) copy-start(f32[1,256]{1,0:T(1,128)} %get-tuple-element.21) | copy-start | bytes 3076
Sparse Core Ops, SparseCore 0:
  9.8 110.3 all-gather.1

commit v2 on v1

--- a/solution.py
+++ b/solution.py
@@ -12,6 +12,9 @@
 ROWS, POOL, D, VOC, FB = 128, 512, 8192, 512, 256
 VMEM_LIMIT = 60 * 1024 * 1024
 N_MSG = 40
+CHUNKS = 2
+SHARD = D // NS
+PIECE = SHARD // CHUNKS
 
 
 def vid(y, x, zh):
@@ -55,7 +58,7 @@
     )
 
 
-def greet(place, sections):
+def greet(place):
     barrier = pltpu.get_barrier_semaphore()
 
     @pl.loop(1, NV)
@@ -64,15 +67,13 @@
             barrier, inc=1, device_id=place.to(lax.rem(place.v + k, NV)), device_id_type=MESH
         )
 
-    if sections:
-
-        @pl.loop(1, NS)
-        def _(k):
-            pl.semaphore_signal(
-                barrier, inc=1, device_id=(lax.rem(place.s + k, NS), place.v), device_id_type=MESH
-            )
-
-    pl.semaphore_wait(barrier, NV - 1 + (NS - 1 if sections else 0))
+    @pl.loop(1, NS)
+    def _(k):
+        pl.semaphore_signal(
+            barrier, inc=1, device_id=(lax.rem(place.s + k, NS), place.v), device_id_type=MESH
+        )
+
+    pl.semaphore_wait(barrier, NV - 1 + NS - 1)
 
 
 def send_stats(place, stats, send_sem, recv_sem):
@@ -149,9 +150,14 @@
             remote(self.buf.at[p.own, 1 - p.zh], self.buf.at[p.own, 1 - p.zh], zsend, zrecv, p.partner()),
         )
 
-    def run(self, zsend, zrecv):
+    def run(self, zsend, zrecv, hooks):
+        def reach(point):
+            if point in hooks:
+                hooks[point]()
+
         out, back = self.partner(zsend, zrecv)
         out.start()
+        reach("start")
         back.wait_recv()
         for half in (0, 1):
             for step in (1, -1):
@@ -159,6 +165,7 @@
         for half in (0, 1):
             for step in (1, -1):
                 self.send(half, 2, 0, 0, 0, "all", step)
+        reach("sent")
         for step, part in ((1, "first"), (-1, "second")):
             for half in (0, 1):
                 self.wait(half, 1, 0, -step, 0, "all", step)
@@ -174,6 +181,7 @@
             self.wait(half, 1, 0, 2, 0, "second", -1)
             for turn in (1, -1):
                 self.send(half, 2, 2, 2, 0, "all", turn)
+        reach("turned")
         for c in (-1, 1, 2):
             for step, part in ((1, "first"), (-1, "second")):
                 for half in (0, 1):
@@ -184,31 +192,122 @@
                 self.wait(half, 2, c, c, 2, "first", 1)
                 self.wait(half, 2, c, c, 2, "second", -1)
         out.wait_send()
+
+    def drain(self):
         for copy in self.sent:
             copy.wait_send()
 
 
-def kernel_a(
-    pick, hidden, final, w_hbm, bias, gain, x_out, lt_out, trans_out, scale_out,
-    xbuf, ltbuf, fbuf, wbuf, stats, acc, w_sem, o_sem, fs, fr, zs, zr, ss1, rs1, ss2, rs2, sts, str_,
+class Table:
+    def __init__(self, place, mine, buf, to_z, to_core, arrived, local):
+        self.place, self.mine, self.buf = place, mine, buf
+        self.to_z, self.to_core, self.arrived, self.local = to_z, to_core, arrived, local
+        self.core = lax.rem(place.s, 2)
+        self.zl = place.s // 2
+
+    def piece(self, shard, part):
+        return self.buf.at[shard, pl.ds(part * PIECE, PIECE), :]
+
+    def along(self, i, part, sign, src=None):
+        shard = 2 * i + self.core
+        here = self.piece(shard, part) if src is None else src
+        return remote(
+            here,
+            self.piece(shard, part),
+            self.to_z.at[0 if sign > 0 else 1, i, part],
+            self.arrived.at[shard, part],
+            (self.place.s + 2 * sign, self.place.v),
+        )
+
+    def across(self, i, part, src=None):
+        shard = 2 * i + self.core
+        here = self.piece(shard, part) if src is None else src
+        return remote(
+            here,
+            self.piece(shard, part),
+            self.to_core.at[i, part],
+            self.arrived.at[shard, part],
+            (self.place.s + 1 - 2 * self.core, self.place.v),
+        )
+
+    def start(self):
+        for part in range(CHUNKS):
+            src = self.mine.at[pl.ds(part * PIECE, PIECE), :]
+
+            @pl.when(self.zl < 3)
+            def _():
+                self.along(self.zl, part, 1, src).start()
+
+            @pl.when(self.zl > 0)
+            def _():
+                self.along(self.zl, part, -1, src).start()
+
+        for part in range(CHUNKS):
+            self.across(self.zl, part, self.mine.at[pl.ds(part * PIECE, PIECE), :]).start()
+        pltpu.make_async_copy(self.mine, self.buf.at[self.place.s], self.local).start()
+
+    def wait(self, shard, part):
+        ref = self.piece(shard, part)
+        remote(ref, ref, self.to_core.at[0, part], self.arrived.at[shard, part], (self.place.s, self.place.v)).wait_recv()
+
+    def relay(self, wave, part):
+        for side in (-1, 1):
+            i = self.zl + side * wave
+            beyond = self.zl - side
+
+            @pl.when((i >= 0) & (i <= 3))
+            def _():
+                self.wait(2 * i + self.core, part)
+
+                @pl.when((beyond >= 0) & (beyond <= 3))
+                def _():
+                    self.along(i, part, -side).start()
+
+                self.across(i, part).start()
+
+    def drain(self):
+        for part in range(CHUNKS):
+            for i in range(4):
+
+                @pl.when((self.zl < 3) & (self.zl >= i))
+                def _():
+                    self.along(i, part, 1).wait_send()
+
+                @pl.when((self.zl > 0) & (self.zl <= i))
+                def _():
+                    self.along(i, part, -1).wait_send()
+
+                self.across(i, part).wait_send()
+
+
+def kernel(
+    pick, hidden, final, w_hbm, bias, gain, u_mine, x_out, dtrans_out, kl_out,
+    xbuf, lt, fbuf, wbuf, u, trans_ref, acc, scale_stats, stats, part, sbuf, rq, rp, rm, r1p, r1m, rz,
+    w_sem, x_sem, u_sem, uz, uc, ua, fs, fr, zs, zr, ss1, rs1, ss2, rs2, ss, rs, sts1, str1, sts2, str2,
 ):
     place = Place()
+    table = Table(place, u_mine, u, uz, uc, ua, u_sem)
     w_copy = pltpu.make_async_copy(w_hbm, wbuf, w_sem)
     w_copy.start()
-    onehot = jnp.where(lax.broadcasted_iota(jnp.int32, (ROWS, POOL), 1) == pick[...], 1.0, 0.0).astype(BF16)
+    chosen = jnp.broadcast_to(pick[...].astype(F32), (ROWS, ROWS)).T[:, 0:1].astype(jnp.int32)
+    onehot = jnp.where(lax.broadcasted_iota(jnp.int32, (ROWS, POOL), 1) == chosen, 1.0, 0.0).astype(BF16)
     inputs = jnp.dot(onehot, hidden[...], preferred_element_type=F32)
     xbuf[place.own, place.zh] = inputs.astype(BF16)
-    greet(place, True)
-
-    @pl.loop(1, NS)
-    def _(k):
-        remote(
-            final, fbuf.at[place.s], fs.at[k], fr.at[place.s], (lax.rem(place.s + k, NS), place.v)
-        ).start()
-
-    fbuf[place.s] = final[...]
-    Gather(place, xbuf, ss1, rs1).run(zs.at[0], zr.at[0])
-    x_copy = pltpu.make_async_copy(xbuf, x_out, o_sem.at[0])
+    greet(place)
+
+    def begin():
+        @pl.loop(1, NS)
+        def _(k):
+            remote(
+                final, fbuf.at[place.s], fs.at[k], fr.at[place.s], (lax.rem(place.s + k, NS), place.v)
+            ).start()
+
+        table.start()
+        fbuf[place.s] = final[...]
+
+    gather_x = Gather(place, xbuf, ss1, rs1)
+    gather_x.run(zs.at[0], zr.at[0], {"start": begin, "turned": lambda: table.relay(1, 0)})
+    x_copy = pltpu.make_async_copy(xbuf, x_out, x_sem)
     x_copy.start()
 
     @pl.loop(1, NS)
@@ -220,59 +319,67 @@
 
     finals = jnp.dot(onehot, fbuf[...].reshape(POOL, FB), preferred_element_type=F32)
     w_copy.wait()
-    acc[...] = xbuf[place.own, place.zh].astype(F32) + bias[...].astype(F32)
+    gain_cols = gain[...].astype(F32).reshape(1, FB)
+    trans_ref[...] = xbuf[place.own, place.zh].astype(F32) + bias[...].astype(F32)
 
     @pl.loop(0, 16)
     def _(p):
         y, x = p // 4, lax.rem(p, 4)
-        total = acc[...]
+        total = trans_ref[...]
         for zh in (0, 1):
             rows = pl.ds(pl.multiple_of(vid(y, x, zh) * FB, FB), FB)
             total = total + jnp.dot(xbuf[p, zh], wbuf[rows, :], preferred_element_type=F32)
-        acc[...] = total
-
-    trans = acc[...]
-    gain_cols = gain[...].astype(F32)
-    ltbuf[place.own, place.zh, 0:ROWS] = (trans * gain_cols).astype(BF16)
-    ltbuf[place.own, place.zh, ROWS : 2 * ROWS] = (finals * gain_cols).astype(BF16)
-    stats[place.v] = to_lanes(
+        trans_ref[...] = total
+
+    trans = trans_ref[...]
+    lt[place.own, place.zh, 0:ROWS] = (trans * gain_cols).astype(BF16)
+    lt[place.own, place.zh, ROWS : 2 * ROWS] = (finals * gain_cols).astype(BF16)
+    scale_stats[place.v] = to_lanes(
         [jnp.sum(trans * trans, axis=1, keepdims=True), jnp.sum(finals * finals, axis=1, keepdims=True)]
     )
-    trans_out[...] = trans
-    send_stats(place, stats, sts, str_)
-    Gather(place, ltbuf, ss2, rs2).run(zs.at[1], zr.at[1])
-    lt_copy = pltpu.make_async_copy(ltbuf, lt_out, o_sem.at[1])
-    lt_copy.start()
-    wait_stats(place, stats, sts, str_)
-    scale_out[...] = lax.rsqrt(jnp.sum(stats[...], axis=0) / D + EPS)
-    x_copy.wait()
-    lt_copy.wait()
-
-
-def kernel_b(
-    lt_hbm, u_hbm, trans, scale, gain, dtrans_out, bias_out, kl_out,
-    lt, u, acc, stats, part, sbuf, rq, rp, rm, r1p, r1m, rz, in_sem, sts, str_, ss, rs, zs, zr,
-):
-    place = Place()
-    chunk = D // 8
-    lt_copy = pltpu.make_async_copy(lt_hbm, lt, in_sem.at[8])
-    lt_copy.start()
-    u_copies = []
-    for i in range(8):
-        rows = pl.ds(i * chunk, chunk)
-        u_copies.append(pltpu.make_async_copy(u_hbm.at[rows], u.at[rows], in_sem.at[i]))
-        u_copies[-1].start()
-    greet(place, False)
-    lt_copy.wait()
-    for i in range(8):
-        u_copies[i].wait()
-        total = acc[...] if i > 0 else None
-        for v in range(4 * i, 4 * i + 4):
-            p, zh = (v // 8) * 4 + v % 4, (v // 4) % 2
-            term = jnp.dot(lt[p, zh], u[v * FB : (v + 1) * FB, :], preferred_element_type=F32)
-            total = term if total is None else total + term
+    send_stats(place, scale_stats, sts1, str1)
+    gather_lt = Gather(place, lt, ss2, rs2)
+    gather_lt.run(
+        zs.at[1], zr.at[1], {"sent": lambda: table.relay(1, 1), "turned": lambda: table.relay(2, 0)}
+    )
+    table.relay(2, 1)
+    acc[...] = jnp.zeros_like(acc)
+
+    def absorb(shard, first, count):
+        total = acc[...]
+        for k in range(first, first + count):
+            total = total + jnp.dot(
+                lt[(shard // 2) * 4 + k, lax.rem(shard, 2)],
+                u[shard, k * FB : (k + 1) * FB, :],
+                preferred_element_type=F32,
+            )
         acc[...] = total
-    columns = to_columns(scale[...])
+
+    pltpu.make_async_copy(u_mine, u.at[place.s], u_sem).wait()
+    absorb(place.s, 0, 4)
+    other = place.s + 1 - 2 * table.core
+    for piece in range(CHUNKS):
+        table.wait(other, piece)
+    absorb(other, 0, 4)
+    for wave in (1, 2, 3):
+        for piece in range(CHUNKS):
+            if wave == 3:
+                table.relay(3, piece)
+            for side in (-1, 1):
+                i = table.zl + side * wave
+
+                @pl.when((i >= 0) & (i <= 3))
+                def _():
+                    per = 4 // CHUNKS
+                    absorb(2 * i + table.core, piece * per, per)
+                    table.wait(2 * i + 1 - table.core, piece)
+                    absorb(2 * i + 1 - table.core, piece * per, per)
+
+    wait_stats(place, scale_stats, sts1, str1)
+    scale = lax.rsqrt(jnp.sum(scale_stats[...], axis=0) / D + EPS)
+
+
+    columns = to_columns(scale)
     trans_scale, final_scale = columns[:, 0:1], columns[:, 1:2]
     logits = acc[0:ROWS] * trans_scale
     target = acc[ROWS : 2 * ROWS] * final_scale
@@ -296,8 +403,8 @@
             jnp.sum(t_exp * l_shift, axis=1, keepdims=True),
         ]
     )
-    send_stats(place, stats, sts, str_)
-    wait_stats(place, stats, sts, str_)
+    send_stats(place, stats, sts2, str2)
+    wait_stats(place, stats, sts2, str2)
     lm, ls, la, tm, ts, ta, tb = (stats[:, k, :] for k in range(7))
 
     def over(values):
@@ -311,7 +418,7 @@
     mean_t = over(tw * (ta + ts * (tm - t_top))) / t_total
     mean_tl = over(tw * (tb + ts * (lm - l_top))) / t_total
     kl_rows = mean_t - mean_tl - jnp.log(t_total) + jnp.log(l_total)
-    kl_out[...] = jnp.broadcast_to(jnp.sum(kl_rows, axis=1, keepdims=True) / ROWS, (8, 128))
+    kl_out[...] = kl_rows
     l_norm = l_top + jnp.log(l_total)
     t_norm = t_top + jnp.log(t_total)
     pull = scale[0:1, :] * (mean_l - mean_tl) / D
@@ -331,9 +438,9 @@
     def product(pair):
         y, x = pair // 4, lax.rem(pair, 4)
         for zh in (0, 1):
-            rows = pl.ds(pl.multiple_of(vid(y, x, zh) * FB, FB), FB)
+            rows = pl.ds(pl.multiple_of(x * FB, FB), FB)
             part[pair, zh] = lax.dot_general(
-                dlogits, u[rows, :], (((1,), (1,)), ((), ())), preferred_element_type=F32
+                dlogits, u[2 * y + zh, rows, :], (((1,), (1,)), ((), ())), preferred_element_type=F32
             )
 
     def move(name, src, dst, device):
@@ -413,112 +520,100 @@
                     total = total + receive(half, 1, 0, 0, 0, "all", step)
                 put(half, 0, 0, "all", total)
                 part[place.own, :, span(half, "all"), :] = total
-    out = remote(sbuf.at[place.own, 1 - place.zh], rz, zs, zr, place.partner())
+    out = remote(sbuf.at[place.own, 1 - place.zh], rz, zs.at[2], zr.at[2], place.partner())
     out.start()
     out.wait_recv()
     dnormed = part[place.own, place.zh] + rz[...].astype(F32)
-    scaled = dnormed * gain[...].astype(F32)
-    dtrans = trans_scale * (scaled - trans[...] * pull)
-    dtrans_out[...] = dtrans.astype(BF16)
-    bias_out[...] = jnp.sum(dtrans, axis=0, keepdims=True)
+    scaled = dnormed * gain_cols
+    dtrans_out[...] = trans_scale * (scaled - trans_ref[...] * pull)
     out.wait_send()
     for copy in sent:
         copy.wait_send()
-
-
-def kernel_c(x, dtrans, out):
-    out[...] = lax.dot_general(
-        x[0, 0], dtrans[...], (((0,), (0,)), ((), ())), preferred_element_type=F32
-    ).astype(BF16)
+    gather_x.drain()
+    gather_lt.drain()
+    table.drain()
+    x_copy.wait()
+
+
+def last_kernel(x, dtrans, kl, grad, grad_bias, kl_mean):
+    rounded = dtrans[...].astype(BF16)
+    for k in range(4):
+        for zh in (0, 1):
+            v = zh * 4 + k
+            grad[v * FB : (v + 1) * FB, :] = lax.dot_general(
+                x[k, zh], rounded, (((0,), (0,)), ((), ())), preferred_element_type=F32
+            ).astype(BF16)
+
+    @pl.when(pl.program_id(0) == 0)
+    def _():
+        grad_bias[...] = jnp.sum(dtrans[...], axis=0, keepdims=True)
+        kl_mean[0] = jnp.sum(kl[...]) / ROWS
 
 
 def per_device(hidden, final_hidden, row_pick, trans_weight, trans_bias, norm_gain, unembed):
-    unembed_full = lax.all_gather(unembed, "section", axis=0, tiled=True)
     whole = pl.BlockSpec(memory_space=pltpu.VMEM)
     anywhere = pl.BlockSpec(memory_space=pl.ANY)
     dma = pltpu.SemaphoreType.DMA
-    gain = norm_gain.reshape(1, FB)
     shape = jax.ShapeDtypeStruct
-    x_all, lt_all, trans, scale = pl.pallas_call(
-        kernel_a,
-        name="gather_rows",
-        out_shape=(
-            shape((16, 2, ROWS, FB), BF16),
-            shape((16, 2, 2 * ROWS, FB), BF16),
-            shape((ROWS, FB), F32),
-            shape((8, 128), F32),
-        ),
-        in_specs=[whole, whole, whole, anywhere, whole, whole],
-        out_specs=(anywhere, anywhere, whole, whole),
+    block = pltpu.VMEM((16, 2, ROWS, FB), BF16)
+    x_all, dtrans, kl = pl.pallas_call(
+        kernel,
+        name="lens",
+        out_shape=(shape((16, 2, ROWS, FB), BF16), shape((ROWS, FB), F32), shape((1, ROWS), F32)),
+        in_specs=[whole, whole, whole, anywhere, whole, whole, anywhere],
+        out_specs=(anywhere, whole, whole),
         scratch_shapes=[
-            pltpu.VMEM((16, 2, ROWS, FB), BF16),
+            block,
             pltpu.VMEM((16, 2, 2 * ROWS, FB), BF16),
             pltpu.VMEM((NS, POOL // NS, FB), BF16),
             pltpu.VMEM((D, FB), BF16),
+            pltpu.VMEM((NS, SHARD, VOC), BF16),
+            pltpu.VMEM((ROWS, FB), F32),
+            pltpu.VMEM((2 * ROWS, VOC), F32),
             pltpu.VMEM((NV, 8, 128), F32),
-            pltpu.VMEM((ROWS, FB), F32),
+            pltpu.VMEM((NV, 8, 128), F32),
+            pltpu.VMEM((16, 2, ROWS, FB), F32),
+            block,
+            block,
+            block,
+            block,
+            pltpu.VMEM((2, ROWS, FB), BF16),
+            pltpu.VMEM((2, ROWS, FB), BF16),
+            pltpu.VMEM((ROWS, FB), BF16),
             dma,
-            dma((2,)),
+            dma,
+            dma,
+            dma((2, 4, CHUNKS)),
+            dma((4, CHUNKS)),
+            dma((NS, CHUNKS)),
             dma((NS,)),
             dma((NS,)),
-            dma((2,)),
-            dma((2,)),
-            dma((N_MSG,)),
-            dma((N_MSG,)),
-            dma((N_MSG,)),
-            dma((N_MSG,)),
-            dma((NV,)),
-            dma((NV,)),
-        ],
+            dma((3,)),
+            dma((3,)),
+        ]
+        + [dma((N_MSG,))] * 6
+        + [dma((NV,))] * 4,
         compiler_params=pltpu.CompilerParams(
             collective_id=0, has_side_effects=True, vmem_limit_bytes=VMEM_LIMIT
         ),
-        cost_estimate=pl.CostEstimate(flops=10**9, bytes_accessed=10**8, transcendentals=0),
-    )(row_pick.reshape(ROWS, 1), hidden[0], final_hidden, trans_weight[0], trans_bias, gain)
-    dtrans, grad_bias, kl = pl.pallas_call(
-        kernel_b,
-        name="softmax_scatter",
-        out_shape=(shape((ROWS, FB), BF16), shape((1, FB), F32), shape((8, 128), F32)),
-        in_specs=[anywhere, anywhere, whole, whole, whole],
-        out_specs=(whole, whole, whole),
-        scratch_shapes=[
-            pltpu.VMEM((16, 2, 2 * ROWS, FB), BF16),
-            pltpu.VMEM((D, VOC), BF16),
-            pltpu.VMEM((2 * ROWS, VOC), F32),
-            pltpu.VMEM((NV, 8, 128), F32),
-            pltpu.VMEM((16, 2, ROWS, FB), F32),
-            pltpu.VMEM((16, 2, ROWS, FB), BF16),
-            pltpu.VMEM((16, 2, ROWS, FB), BF16),
-            pltpu.VMEM((16, 2, ROWS, FB), BF16),
-            pltpu.VMEM((16, 2, ROWS, FB), BF16),
-            pltpu.VMEM((2, ROWS, FB), BF16),
-            pltpu.VMEM((2, ROWS, FB), BF16),
-            pltpu.VMEM((ROWS, FB), BF16),
-            dma((9,)),
-            dma((NV,)),
-            dma((NV,)),
-            dma((N_MSG,)),
-            dma((N_MSG,)),
-            dma,
-            dma,
+    )(row_pick, hidden[0], final_hidden, trans_weight[0], trans_bias, norm_gain, unembed)
+    grad_weight, grad_bias, kl_mean = pl.pallas_call(
+        last_kernel,
+        name="weight_gradient",
+        grid=(4,),
+        out_shape=(shape((D, FB), BF16), shape((1, FB), F32), shape((1,), F32)),
+        in_specs=[
+            pl.BlockSpec((4, 2, ROWS, FB), lambda y: (y, 0, 0, 0)),
+            pl.BlockSpec((ROWS, FB), lambda y: (0, 0)),
+            pl.BlockSpec((1, ROWS), lambda y: (0, 0)),
         ],
-        compiler_params=pltpu.CompilerParams(
-            collective_id=1, has_side_effects=True, vmem_limit_bytes=VMEM_LIMIT
+        out_specs=(
+            pl.BlockSpec((D // 4, FB), lambda y: (y, 0)),
+            pl.BlockSpec((1, FB), lambda y: (0, 0)),
+            pl.BlockSpec(memory_space=pltpu.SMEM),
         ),
-        cost_estimate=pl.CostEstimate(flops=10**9, bytes_accessed=10**8, transcendentals=0),
-    )(lt_all, unembed_full, trans, scale, gain)
-    grad_weight = pl.pallas_call(
-        kernel_c,
-        name="weight_gradient",
-        grid=(NV,),
-        out_shape=shape((D, FB), BF16),
-        in_specs=[
-            pl.BlockSpec((1, 1, ROWS, FB), lambda v: ((v // 8) * 4 + v % 4, (v // 4) % 2, 0, 0)),
-            pl.BlockSpec((ROWS, FB), lambda v: (0, 0)),
-        ],
-        out_specs=pl.BlockSpec((FB, FB), lambda v: (v, 0)),
-    )(x_all, dtrans)
-    return grad_weight[None], grad_bias, kl[0, 0:1]
+    )(x_all, dtrans, kl)
+    return grad_weight[None], grad_bias, kl_mean
 
 
 def solution(mesh):

time: 190 us -> 144 us (0.76); the launches traced: 187 us -> 143 us
  waiting for transfers between devices: 21.1 us -> 0 us
  between operations: 14.1 us -> 0.64 us
  local copies, waits for them, and re-layouts: 4.36 us -> 0 us
  Pallas kernels: 147 us -> 143 us
    all_gather x1 -> x0, waiting for transfers between devices: 20.4 us -> none  [per_device(): unembed_full = lax.all_gather(unembed, 'section', axis=0, tiled=True)]
    pallas_call x3 -> x2, Pallas kernels: 147 us -> 143 us  [the longest x1 138 us: per_device(): pl.pallas_call(kernel, name='lens', out_shape=(shape((16, 2, ROWS, FB), B...]
    reshape x2 -> x0, local copies, waits for them, and re-layouts: 2.61 us -> none  [the longest x1 1.39 us: per_device(): row_pick.reshape(ROWS, 1)]
  transfers between devices with their start and end apart: 1 -> 0, of which waited for: 1 -> 0; matrix products, arithmetic and copies ran while one was open for 1% -> 0% of each run, Pallas kernels for 48% -> 0%
where the time goes in v2:
time: 144 us; the launch traced here: 143 us
  Pallas kernels  143 us (99%)
    pallas_call x1, Pallas kernels, per_device(): pl.pallas_call(kernel, name='lens', out_shape=(shape((16, 2, ROWS, FB), B...  138 us
    pallas_call x1, Pallas kernels, per_device(): pl.pallas_call(last_kernel, name='weight_gradient', grid=(4,), out_shape=...  5.14 us

profile of v2, /device:TPU:2, one launch (start us, length us, event | category | flops | bytes accessed | tf_op | source)
XLA Modules:
  0.0 143.3 jit_solution(10107036225657661065)
XLA Ops:
  0.6 137.5 %lens.1 = (bf16[16,2,128,256]{3,2,1,0:T(8,128)(2,1)}, f32[128,256]{1,0:T(8,128)}, f32[1,128]{1,0:T(1,128)}) custom-call(s32[1,128]{1,0:T(1,128)} %pick.1, bf16[512,256]{1,0:T(8,128)(2,1)} %bitcast.4, bf16[64,256]{1,0:T(8,128)(2,1)} %final.1, bf16[8192,256]{1,0:T(8,128)(2,1)} %bitcast.3, bf16[1,256]{1,0:T(2,128)(2,1)} %bias.1, bf16[256]{0:T(256)(128)(2,1)} %gain.1, ...), custom_call_target="tpu_custom_call" | custom-call | tf_op jit(solution)/shard_map/lens/pallas_call | solution.py:559
  138.2 5.1 %weight_gradient.1 = (bf16[8192,256]{1,0:T(8,128)(2,1)}, f32[1,256]{1,0:T(1,128)}, f32[1]{0:T(128)}) custom-call(bf16[16,2,128,256]{3,2,1,0:T(8,128)(2,1)} %get-tuple-element.9.x, f32[128,256]{1,0:T(8,128)} %get-tuple-element.10.dtrans, f32[1,128]{1,0:T(1,128)} %get-tuple-element.11.kl), custom_call_target="tpu_custom_call" | custom-call | tf_op jit(solution)/shard_map/weight_gradient/pallas_call | solution.py:600

commit v3 on v2

--- a/solution.py
+++ b/solution.py
@@ -40,6 +40,15 @@
     def partner(self):
         return self.to(vid(self.y, self.x, 1 - self.zh))
 
+    def along_z(self, step):
+        z = lax.rem(self.zh * 4 + self.s // 2 + (step + 8), 8)
+        return (lax.rem(z, 4) * 2 + lax.rem(self.s, 2), vid(self.y, self.x, z // 4))
+
+    def touching(self):
+        across = (self.s + 1 - 2 * lax.rem(self.s, 2), self.v)
+        sides = [self.near(half, 1, step) for half in (0, 1) for step in (1, -1)]
+        return sides + [self.along_z(1), self.along_z(-1), across]
+
     def near(self, half, stage, step):
         along_x = (half == 0) == (stage == 1)
         if along_x:
@@ -58,22 +67,23 @@
     )
 
 
-def greet(place):
+def announce(place):
     barrier = pltpu.get_barrier_semaphore()
-
-    @pl.loop(1, NV)
-    def _(k):
+    for device in place.touching():
+        pl.semaphore_signal(barrier, inc=1, device_id=device, device_id_type=MESH)
+
+
+def await_touching(place):
+    pl.semaphore_wait(pltpu.get_barrier_semaphore(), len(place.touching()))
+
+
+def widen(place, known, turn):
+    for side in (0, 1):
         pl.semaphore_signal(
-            barrier, inc=1, device_id=place.to(lax.rem(place.v + k, NV)), device_id_type=MESH
+            known.at[turn, side], inc=1, device_id=place.along_z(1 - 2 * side), device_id_type=MESH
         )
-
-    @pl.loop(1, NS)
-    def _(k):
-        pl.semaphore_signal(
-            barrier, inc=1, device_id=(lax.rem(place.s + k, NS), place.v), device_id_type=MESH
-        )
-
-    pl.semaphore_wait(barrier, NV - 1 + NS - 1)
+    for side in (0, 1):
+        pl.semaphore_wait(known.at[turn, side], 1)
 
 
 def send_stats(place, stats, send_sem, recv_sem):
@@ -280,46 +290,89 @@
                 self.across(i, part).wait_send()
 
 
+class Finals:
+    def __init__(self, place, mine, buf, to_z, to_core, arrived):
+        self.place, self.mine, self.buf = place, mine, buf
+        self.to_z, self.to_core, self.arrived = to_z, to_core, arrived
+        self.core = lax.rem(place.s, 2)
+        self.zl = place.s // 2
+
+    def along(self, k):
+        i = lax.rem(self.zl + k, 4)
+        return remote(
+            self.mine,
+            self.buf.at[self.place.s],
+            self.to_z.at[k],
+            self.arrived.at[self.place.s],
+            (2 * i + self.core, self.place.v),
+        )
+
+    def across(self, k):
+        shard = 2 * lax.rem(self.zl + k, 4) + self.core
+        here = self.mine if k == 0 else self.buf.at[shard]
+        return remote(
+            here,
+            self.buf.at[shard],
+            self.to_core.at[k],
+            self.arrived.at[shard],
+            (self.place.s + 1 - 2 * self.core, self.place.v),
+        )
+
+    def wait(self, shard):
+        ref = self.buf.at[shard]
+        remote(ref, ref, self.to_core.at[0], self.arrived.at[shard], (self.place.s, self.place.v)).wait_recv()
+
+    def start(self):
+        for k in (1, 2, 3):
+            self.along(k).start()
+        self.across(0).start()
+
+    def forward(self):
+        for k in (1, 2, 3):
+            self.wait(2 * lax.rem(self.zl + k, 4) + self.core)
+            self.across(k).start()
+
+    def finish(self):
+        for k in range(4):
+            self.wait(2 * lax.rem(self.zl + k, 4) + 1 - self.core)
+
+    def drain(self):
+        for k in (1, 2, 3):
+            self.along(k).wait_send()
+        for k in range(4):
+            self.across(k).wait_send()
+
+
 def kernel(
-    pick, hidden, final, w_hbm, bias, gain, u_mine, x_out, dtrans_out, kl_out,
-    xbuf, lt, fbuf, wbuf, u, trans_ref, acc, scale_stats, stats, part, sbuf, rq, rp, rm, r1p, r1m, rz,
-    w_sem, x_sem, u_sem, uz, uc, ua, fs, fr, zs, zr, ss1, rs1, ss2, rs2, ss, rs, sts1, str1, sts2, str2,
+    pick, hidden_hbm, final_hbm, w_hbm, bias, gain, u_mine, x_out, dtrans_out, kl_out,
+    hidden, xbuf, xt, lt, fbuf, wbuf, u, trans_ref, acc, scale_stats, stats, part, sbuf, rq, rp, rm, r1p, r1m, rz,
+    in_sem, x_sem, u_sem, uz, uc, ua, fz, fc, fa, known, zs, zr, ss1, rs1, ss2, rs2, ss, rs, sts1, str1, sts2, str2,
 ):
     place = Place()
+    announce(place)
     table = Table(place, u_mine, u, uz, uc, ua, u_sem)
-    w_copy = pltpu.make_async_copy(w_hbm, wbuf, w_sem)
+    pool = Finals(place, final_hbm, fbuf, fz, fc, fa)
+    hidden_copy = pltpu.make_async_copy(hidden_hbm, hidden, in_sem.at[0])
+    hidden_copy.start()
+    final_copy = pltpu.make_async_copy(final_hbm, fbuf.at[place.s], in_sem.at[1])
+    final_copy.start()
+    w_copy = pltpu.make_async_copy(w_hbm, wbuf, in_sem.at[2])
     w_copy.start()
     chosen = jnp.broadcast_to(pick[...].astype(F32), (ROWS, ROWS)).T[:, 0:1].astype(jnp.int32)
     onehot = jnp.where(lax.broadcasted_iota(jnp.int32, (ROWS, POOL), 1) == chosen, 1.0, 0.0).astype(BF16)
+    await_touching(place)
+    table.start()
+    hidden_copy.wait()
     inputs = jnp.dot(onehot, hidden[...], preferred_element_type=F32)
     xbuf[place.own, place.zh] = inputs.astype(BF16)
-    greet(place)
-
-    def begin():
-        @pl.loop(1, NS)
-        def _(k):
-            remote(
-                final, fbuf.at[place.s], fs.at[k], fr.at[place.s], (lax.rem(place.s + k, NS), place.v)
-            ).start()
-
-        table.start()
-        fbuf[place.s] = final[...]
-
+    for turn in range(3):
+        widen(place, known, turn)
     gather_x = Gather(place, xbuf, ss1, rs1)
-    gather_x.run(zs.at[0], zr.at[0], {"start": begin, "turned": lambda: table.relay(1, 0)})
-    x_copy = pltpu.make_async_copy(xbuf, x_out, x_sem)
-    x_copy.start()
-
-    @pl.loop(1, NS)
-    def _(k):
-        src = lax.rem(place.s + k, NS)
-        copy = remote(fbuf.at[src], fbuf.at[src], fs.at[k], fr.at[src], (src, place.v))
-        copy.wait_send()
-        copy.wait_recv()
-
-    finals = jnp.dot(onehot, fbuf[...].reshape(POOL, FB), preferred_element_type=F32)
+    gather_x.run(zs.at[0], zr.at[0], {"start": pool.start, "turned": lambda: table.relay(1, 0)})
+    final_copy.wait()
+    pool.forward()
+    gain_cols = gain[...].astype(F32).reshape(1, FB)
     w_copy.wait()
-    gain_cols = gain[...].astype(F32).reshape(1, FB)
     trans_ref[...] = xbuf[place.own, place.zh].astype(F32) + bias[...].astype(F32)
 
     @pl.loop(0, 16)
@@ -331,6 +384,8 @@
             total = total + jnp.dot(xbuf[p, zh], wbuf[rows, :], preferred_element_type=F32)
         trans_ref[...] = total
 
+    pool.finish()
+    finals = jnp.dot(onehot, fbuf[...].reshape(POOL, FB), preferred_element_type=F32)
     trans = trans_ref[...]
     lt[place.own, place.zh, 0:ROWS] = (trans * gain_cols).astype(BF16)
     lt[place.own, place.zh, ROWS : 2 * ROWS] = (finals * gain_cols).astype(BF16)
@@ -362,6 +417,15 @@
         table.wait(other, piece)
     absorb(other, 0, 4)
     for wave in (1, 2, 3):
+        if wave == 3:
+
+            @pl.loop(0, 16)
+            def _(p):
+                for zh in (0, 1):
+                    xt[p, zh] = xbuf[p, zh].astype(F32).T.astype(BF16)
+
+            x_copy = pltpu.make_async_copy(xt, x_out, x_sem)
+            x_copy.start()
         for piece in range(CHUNKS):
             if wave == 3:
                 table.relay(3, piece)
@@ -532,6 +596,7 @@
     gather_x.drain()
     gather_lt.drain()
     table.drain()
+    pool.drain()
     x_copy.wait()
 
 
@@ -541,7 +606,7 @@
         for zh in (0, 1):
             v = zh * 4 + k
             grad[v * FB : (v + 1) * FB, :] = lax.dot_general(
-                x[k, zh], rounded, (((0,), (0,)), ((), ())), preferred_element_type=F32
+                x[k, zh], rounded, (((1,), (0,)), ((), ())), preferred_element_type=F32
             ).astype(BF16)
 
     @pl.when(pl.program_id(0) == 0)
@@ -559,11 +624,13 @@
     x_all, dtrans, kl = pl.pallas_call(
         kernel,
         name="lens",
-        out_shape=(shape((16, 2, ROWS, FB), BF16), shape((ROWS, FB), F32), shape((1, ROWS), F32)),
-        in_specs=[whole, whole, whole, anywhere, whole, whole, anywhere],
+        out_shape=(shape((16, 2, FB, ROWS), BF16), shape((ROWS, FB), F32), shape((1, ROWS), F32)),
+        in_specs=[whole, anywhere, anywhere, anywhere, whole, whole, anywhere],
         out_specs=(anywhere, whole, whole),
         scratch_shapes=[
+            pltpu.VMEM((POOL, FB), BF16),
             block,
+            pltpu.VMEM((16, 2, FB, ROWS), BF16),
             pltpu.VMEM((16, 2, 2 * ROWS, FB), BF16),
             pltpu.VMEM((NS, POOL // NS, FB), BF16),
             pltpu.VMEM((D, FB), BF16),
@@ -580,14 +647,16 @@
             pltpu.VMEM((2, ROWS, FB), BF16),
             pltpu.VMEM((2, ROWS, FB), BF16),
             pltpu.VMEM((ROWS, FB), BF16),
-            dma,
+            dma((3,)),
             dma,
             dma,
             dma((2, 4, CHUNKS)),
             dma((4, CHUNKS)),
             dma((NS, CHUNKS)),
+            dma((4,)),
+            dma((4,)),
             dma((NS,)),
-            dma((NS,)),
+            pltpu.SemaphoreType.REGULAR((3, 2)),
             dma((3,)),
             dma((3,)),
         ]
@@ -603,7 +672,7 @@
         grid=(4,),
         out_shape=(shape((D, FB), BF16), shape((1, FB), F32), shape((1,), F32)),
         in_specs=[
-            pl.BlockSpec((4, 2, ROWS, FB), lambda y: (y, 0, 0, 0)),
+            pl.BlockSpec((4, 2, FB, ROWS), lambda y: (y, 0, 0, 0)),
             pl.BlockSpec((ROWS, FB), lambda y: (0, 0)),
             pl.BlockSpec((1, ROWS), lambda y: (0, 0)),
         ],

time: 144 us -> 144 us (level)
  no operation moved by 1% of the time
where the time goes in v3:
time: 144 us; the launch traced here: 143 us
  Pallas kernels  143 us (99%)
    pallas_call x1, Pallas kernels, per_device(): pl.pallas_call(kernel, name='lens', out_shape=(shape((16, 2, FB, ROWS), B...  138 us
    pallas_call x1, Pallas kernels, per_device(): pl.pallas_call(last_kernel, name='weight_gradient', grid=(4,), out_shape=...  5.04 us

profile of v3, /device:TPU:2, one launch (start us, length us, event | category | flops | bytes accessed | tf_op | source)
XLA Modules:
  0.0 143.2 jit_solution(13265211999511790778)
XLA Ops:
  0.6 137.5 %lens.1 = (bf16[16,2,256,128]{3,2,1,0:T(8,128)(2,1)}, f32[128,256]{1,0:T(8,128)}, f32[1,128]{1,0:T(1,128)}) custom-call(s32[1,128]{1,0:T(1,128)} %pick.1, bf16[512,256]{1,0:T(8,128)(2,1)} %bitcast.4, bf16[64,256]{1,0:T(8,128)(2,1)} %final_hbm.1, bf16[8192,256]{1,0:T(8,128)(2,1)} %bitcast.3, bf16[1,256]{1,0:T(2,128)(2,1)} %bias.1, bf16[256]{0:T(256)(128)(2,1)} %gain.1, ...), custom_call_target="tpu_custom_call" | custom-call | tf_op jit(solution)/shard_map/lens/pallas_call | solution.py:624
  138.2 5.0 %weight_gradient.1 = (bf16[8192,256]{1,0:T(8,128)(2,1)}, f32[1,256]{1,0:T(1,128)}, f32[1]{0:T(128)}) custom-call(bf16[16,2,256,128]{3,2,1,0:T(8,128)(2,1)} %get-tuple-element.9.x, f32[128,256]{1,0:T(8,128)} %get-tuple-element.10.dtrans, f32[1,128]{1,0:T(1,128)} %get-tuple-element.11.kl), custom_call_target="tpu_custom_call" | custom-call | tf_op jit(solution)/shard_map/weight_gradient/pallas_call | solution.py:669

commit v4 on v3

--- a/solution.py
+++ b/solution.py
@@ -11,8 +11,9 @@
 NV, NS = 32, 8
 ROWS, POOL, D, VOC, FB = 128, 512, 8192, 512, 256
 VMEM_LIMIT = 60 * 1024 * 1024
-N_MSG = 40
-CHUNKS = 2
+N_MSG = 30
+STEPS = (1, -1, 2)
+CHUNKS = 4
 SHARD = D // NS
 PIECE = SHARD // CHUNKS
 
@@ -75,6 +76,20 @@
 
 def await_touching(place):
     pl.semaphore_wait(pltpu.get_barrier_semaphore(), len(place.touching()))
+
+
+def widen_plane(place, known):
+    for half in (0, 1):
+        for side in (0, 1):
+            pl.semaphore_signal(
+                known.at[3 + half, side],
+                inc=1,
+                device_id=place.near(half, 1, 1 - 2 * side),
+                device_id_type=MESH,
+            )
+    for half in (0, 1):
+        for side in (0, 1):
+            pl.semaphore_wait(known.at[3 + half, side], 1)
 
 
 def widen(place, known, turn):
@@ -119,93 +134,123 @@
     return jnp.concatenate([tile, jnp.zeros((120, 128), F32)], axis=0).T
 
 
-class Gather:
-    ORDER = (0, -1, 1, 2)
-
-    def __init__(self, place, buf, send_sem, recv_sem):
-        self.place, self.buf, self.ss, self.rs = place, buf, send_sem, recv_sem
-        self.rows = buf.shape[2]
+class Plane:
+    def __init__(self, place, buf, level, base, send_sem, recv_sem):
+        self.place, self.buf, self.level, self.base = place, buf, level, base
+        self.ss, self.rs = send_sem, recv_sem
         self.sent = []
         self.ids = {}
 
-    def span(self, half, part):
-        h, q = self.rows // 2, self.rows // 4
-        if part == "all":
-            return pl.ds(half * h, h)
-        return pl.ds(half * h + (0 if part == "first" else q), q)
-
-    def key(self, *name):
-        return self.ids.setdefault(name, len(self.ids))
-
-    def move(self, name, pair, half, part, device):
-        ref = self.buf.at[pair, :, self.span(half, part), :]
-        k = self.key(*name)
+    def move(self, name, pair, half, device):
+        rows = pl.ds(self.base + half * (ROWS // 2), ROWS // 2)
+        ref = self.buf.at[pair, self.level, rows, :]
+        k = self.ids.setdefault(name, len(self.ids))
         return remote(ref, ref, self.ss.at[k], self.rs.at[k], device)
 
-    def send(self, half, stage, col, c, d, part, step):
+    def first(self, half, c):
         p = self.place
-        copy = self.move((half, stage, col, part, step), p.pair(half, c, d), half, part, p.near(half, stage, step))
-        copy.start()
-        self.sent.append(copy)
-
-    def wait(self, half, stage, col, c, d, part, step):
+        self.sent.append(self.move((half, c), p.own, half, p.near(half, 1, c)))
+        self.sent[-1].start()
+
+    def second(self, half, c, d):
         p = self.place
-        self.move((half, stage, col, part, step), p.pair(half, c, d), half, part, p.near(half, stage, -step)).wait_recv()
-
-    def partner(self, zsend, zrecv):
+        self.sent.append(self.move((half, c, d), p.pair(half, -c, 0), half, p.near(half, 2, d)))
+        self.sent[-1].start()
+
+    def steps(self):
         p = self.place
-        mine = self.buf.at[p.own, p.zh]
-        return (
-            remote(mine, mine, zsend, zrecv, p.partner()),
-            remote(self.buf.at[p.own, 1 - p.zh], self.buf.at[p.own, 1 - p.zh], zsend, zrecv, p.partner()),
-        )
-
-    def run(self, zsend, zrecv, hooks):
-        def reach(point):
-            if point in hooks:
-                hooks[point]()
-
-        out, back = self.partner(zsend, zrecv)
-        out.start()
-        reach("start")
-        back.wait_recv()
-        for half in (0, 1):
-            for step in (1, -1):
-                self.send(half, 1, 0, 0, 0, "all", step)
-        for half in (0, 1):
-            for step in (1, -1):
-                self.send(half, 2, 0, 0, 0, "all", step)
-        reach("sent")
-        for step, part in ((1, "first"), (-1, "second")):
+        for c in STEPS:
             for half in (0, 1):
-                self.wait(half, 1, 0, -step, 0, "all", step)
-                self.send(half, 1, 0, -step, 0, part, step)
-                for turn in (1, -1):
-                    self.send(half, 2, -step, -step, 0, "all", turn)
-        for step, part in ((1, "first"), (-1, "second")):
+                self.first(half, c)
+        for d in STEPS:
             for half in (0, 1):
-                self.wait(half, 2, 0, 0, -step, "all", step)
-                self.send(half, 2, 0, 0, -step, part, step)
-        for half in (0, 1):
-            self.wait(half, 1, 0, 2, 0, "first", 1)
-            self.wait(half, 1, 0, 2, 0, "second", -1)
-            for turn in (1, -1):
-                self.send(half, 2, 2, 2, 0, "all", turn)
-        reach("turned")
-        for c in (-1, 1, 2):
-            for step, part in ((1, "first"), (-1, "second")):
-                for half in (0, 1):
-                    self.wait(half, 2, c, c, -step, "all", step)
-                    self.send(half, 2, c, c, -step, part, step)
-        for c in self.ORDER:
+                self.second(half, 0, d)
+        yield
+        for c in STEPS:
             for half in (0, 1):
-                self.wait(half, 2, c, c, 2, "first", 1)
-                self.wait(half, 2, c, c, 2, "second", -1)
-        out.wait_send()
+                self.move((half, c), p.pair(half, -c, 0), half, p.near(half, 1, -c)).wait_recv()
+                for d in STEPS:
+                    self.second(half, c, d)
+            yield
+        for c in (0,) + STEPS:
+            for half in (0, 1):
+                for d in STEPS:
+                    self.move((half, c, d), p.pair(half, -c, -d), half, p.near(half, 2, -d)).wait_recv()
+        yield
 
     def drain(self):
         for copy in self.sent:
             copy.wait_send()
+
+
+class Scatter:
+    def __init__(self, place, level, product, refs, send_sem, recv_sem):
+        self.place, self.level, self.product = place, level, product
+        self.part, self.sbuf, self.arrive, self.last = refs
+        self.ss, self.rs = send_sem, recv_sem
+        self.sent = []
+        self.ids = {}
+
+    def rows(self, half):
+        return pl.ds(half * (ROWS // 2), ROWS // 2)
+
+    def landing(self, name, pair):
+        if len(name) == 3:
+            return self.arrive[STEPS.index(name[2])].at[pair, self.level, self.rows(name[0]), :]
+        return self.last[STEPS.index(name[1])].at[self.level, self.rows(name[0]), :]
+
+    def move(self, name, src, dst, device):
+        k = self.ids.setdefault(name, len(self.ids))
+        return remote(src, dst, self.ss.at[k], self.rs.at[k], device)
+
+    def send(self, name, pair, device, value):
+        half = name[0]
+        self.sbuf[pair, self.level, self.rows(half), :] = value.astype(BF16)
+        src = self.sbuf.at[pair, self.level, self.rows(half), :]
+        self.sent.append(self.move(name, src, self.landing(name, pair), device))
+        self.sent[-1].start()
+
+    def receive(self, name, pair, device):
+        ref = self.landing(name, pair)
+        self.move(name, ref, ref, device).wait_recv()
+        return ref[...].astype(F32)
+
+    def mine(self, half, c, d):
+        return self.part[self.place.pair(half, c, d), self.level, self.rows(half), :]
+
+    def open(self):
+        p = self.place
+        order = [(a, b) for a in (2, 1, -1) for b in (2, 1, -1)]
+        order += [(a, 0) for a in (2, 1, -1)] + [(0, b) for b in (2, 1, -1)] + [(0, 0)]
+        for dx, dy in order:
+            pair = p.pair(0, dx, dy)
+            self.product(pair, self.level)
+            for half in (0, 1):
+                c, d = (dx, dy) if half == 0 else (dy, dx)
+                if d != 0:
+                    self.send((half, c, d), pair, p.near(half, 2, d), self.mine(half, c, d))
+
+    def column(self, half, c):
+        p = self.place
+        total = self.mine(half, c, 0)
+        for d in STEPS:
+            total = total + self.receive((half, c, d), p.pair(half, c, 0), p.near(half, 2, -d))
+        return total
+
+    def turn(self):
+        p = self.place
+        for c in (2, 1, -1):
+            for half in (0, 1):
+                self.send((half, c), p.pair(half, c, 0), p.near(half, 1, c), self.column(half, c))
+
+    def close(self):
+        p = self.place
+        for half in (0, 1):
+            total = self.column(half, 0)
+            for c in STEPS:
+                total = total + self.receive((half, c), p.own, p.near(half, 1, -c))
+            self.sbuf[p.own, self.level, self.rows(half), :] = total.astype(BF16)
+            self.part[p.own, self.level, self.rows(half), :] = total
 
 
 class Table:
@@ -240,8 +285,8 @@
             (self.place.s + 1 - 2 * self.core, self.place.v),
         )
 
-    def start(self):
-        for part in range(CHUNKS):
+    def start(self, parts):
+        for part in parts:
             src = self.mine.at[pl.ds(part * PIECE, PIECE), :]
 
             @pl.when(self.zl < 3)
@@ -252,9 +297,7 @@
             def _():
                 self.along(self.zl, part, -1, src).start()
 
-        for part in range(CHUNKS):
-            self.across(self.zl, part, self.mine.at[pl.ds(part * PIECE, PIECE), :]).start()
-        pltpu.make_async_copy(self.mine, self.buf.at[self.place.s], self.local).start()
+            self.across(self.zl, part, src).start()
 
     def wait(self, shard, part):
         ref = self.piece(shard, part)
@@ -345,8 +388,8 @@
 
 def kernel(
     pick, hidden_hbm, final_hbm, w_hbm, bias, gain, u_mine, x_out, dtrans_out, kl_out,
-    hidden, xbuf, xt, lt, fbuf, wbuf, u, trans_ref, acc, scale_stats, stats, part, sbuf, rq, rp, rm, r1p, r1m, rz,
-    in_sem, x_sem, u_sem, uz, uc, ua, fz, fc, fa, known, zs, zr, ss1, rs1, ss2, rs2, ss, rs, sts1, str1, sts2, str2,
+    hidden, xbuf, xt, lt, fbuf, wbuf, u, trans_ref, acc, scale_stats, stats, part, sbuf, rq, rp, rm, r1p, r1m, r1q, rz,
+    in_sem, x_sem, u_sem, uz, uc, ua, fz, fc, fa, known, zs, zr, pss, prs, ss, rs, sts1, str1, sts2, str2,
 ):
     place = Place()
     announce(place)
@@ -360,44 +403,99 @@
     w_copy.start()
     chosen = jnp.broadcast_to(pick[...].astype(F32), (ROWS, ROWS)).T[:, 0:1].astype(jnp.int32)
     onehot = jnp.where(lax.broadcasted_iota(jnp.int32, (ROWS, POOL), 1) == chosen, 1.0, 0.0).astype(BF16)
+    gain_cols = gain[...].astype(F32).reshape(1, FB)
+
+    planes = []
+
+    def plane(buf, level, base):
+        k = len(planes)
+        planes.append(Plane(place, buf, level, base, pss.at[k], prs.at[k]))
+        return planes[-1].steps()
+
+    def go(steps, count=1):
+        for _ in range(count):
+            next(steps)
+
+    def crossing(buf, base, k, level):
+        ref = buf.at[place.own, level, pl.ds(base, ROWS), :]
+        return remote(ref, ref, zs.at[k], zr.at[k], place.partner())
+
+    near_x, far_x = plane(xbuf, place.zh, 0), plane(xbuf, 1 - place.zh, 0)
+    near_t, far_t = plane(lt, place.zh, ROWS), plane(lt, 1 - place.zh, ROWS)
+    near_l, far_l = plane(lt, place.zh, 0), plane(lt, 1 - place.zh, 0)
+
+    def multiply(level):
+        @pl.loop(0, 4)
+        def _(y):
+            total = trans_ref[...]
+            for x in range(4):
+                rows = pl.ds(pl.multiple_of(vid(y, x, level) * FB, FB), FB)
+                total = total + jnp.dot(xbuf[y * 4 + x, level], wbuf[rows, :], preferred_element_type=F32)
+            trans_ref[...] = total
+
     await_touching(place)
-    table.start()
+    table.start((0, 1))
     hidden_copy.wait()
     inputs = jnp.dot(onehot, hidden[...], preferred_element_type=F32)
     xbuf[place.own, place.zh] = inputs.astype(BF16)
-    for turn in range(3):
-        widen(place, known, turn)
-    gather_x = Gather(place, xbuf, ss1, rs1)
-    gather_x.run(zs.at[0], zr.at[0], {"start": pool.start, "turned": lambda: table.relay(1, 0)})
+    trans_ref[...] = inputs + bias[...].astype(F32)
+    widen_plane(place, known)
+    go(near_x)
+    widen(place, known, 0)
+    go(near_x, 2)
+    widen(place, known, 1)
+    pool.start()
+    go(near_x)
+    widen(place, known, 2)
+    cross_x = crossing(xbuf, 0, 0, place.zh)
+    cross_x.start()
+    table.start((2, 3))
+    u_copy = pltpu.make_async_copy(u_mine, u.at[place.s], u_sem)
+    u_copy.start()
+    go(near_x)
+    crossing(xbuf, 0, 0, 1 - place.zh).wait_recv()
+    go(far_x)
     final_copy.wait()
     pool.forward()
-    gain_cols = gain[...].astype(F32).reshape(1, FB)
-    w_copy.wait()
-    trans_ref[...] = xbuf[place.own, place.zh].astype(F32) + bias[...].astype(F32)
-
-    @pl.loop(0, 16)
-    def _(p):
-        y, x = p // 4, lax.rem(p, 4)
-        total = trans_ref[...]
-        for zh in (0, 1):
-            rows = pl.ds(pl.multiple_of(vid(y, x, zh) * FB, FB), FB)
-            total = total + jnp.dot(xbuf[p, zh], wbuf[rows, :], preferred_element_type=F32)
-        trans_ref[...] = total
-
+    go(far_x, 3)
+    table.relay(1, 0)
     pool.finish()
     finals = jnp.dot(onehot, fbuf[...].reshape(POOL, FB), preferred_element_type=F32)
+    lt[place.own, place.zh, ROWS : 2 * ROWS] = (finals * gain_cols).astype(BF16)
+    cross_t = crossing(lt, ROWS, 1, place.zh)
+    cross_t.start()
+    go(near_t)
+    w_copy.wait()
+    multiply(place.zh)
+    table.relay(1, 1)
+    go(near_t, 3)
+    go(far_x)
+    multiply(1 - place.zh)
     trans = trans_ref[...]
     lt[place.own, place.zh, 0:ROWS] = (trans * gain_cols).astype(BF16)
-    lt[place.own, place.zh, ROWS : 2 * ROWS] = (finals * gain_cols).astype(BF16)
+    cross_l = crossing(lt, 0, 2, place.zh)
+    cross_l.start()
+    go(near_l)
     scale_stats[place.v] = to_lanes(
         [jnp.sum(trans * trans, axis=1, keepdims=True), jnp.sum(finals * finals, axis=1, keepdims=True)]
     )
     send_stats(place, scale_stats, sts1, str1)
-    gather_lt = Gather(place, lt, ss2, rs2)
-    gather_lt.run(
-        zs.at[1], zr.at[1], {"sent": lambda: table.relay(1, 1), "turned": lambda: table.relay(2, 0)}
-    )
+    table.relay(1, 2)
+    go(near_l, 3)
+    crossing(lt, ROWS, 1, 1 - place.zh).wait_recv()
+    go(far_t)
+    table.relay(1, 3)
+    go(far_t, 3)
+    crossing(lt, 0, 2, 1 - place.zh).wait_recv()
+    go(far_l)
+    table.relay(2, 0)
+    go(far_l, 3)
+    go(near_t)
+    go(near_l)
     table.relay(2, 1)
+    go(far_t)
+    go(far_l)
+    table.relay(2, 2)
     acc[...] = jnp.zeros_like(acc)
 
     def absorb(shard, first, count):
@@ -410,35 +508,42 @@
             )
         acc[...] = total
 
-    pltpu.make_async_copy(u_mine, u.at[place.s], u_sem).wait()
-    absorb(place.s, 0, 4)
-    other = place.s + 1 - 2 * table.core
+    def each_side(wave, then):
+        for side in (-1, 1):
+            i = table.zl + side * wave
+
+            @pl.when((i >= 0) & (i <= 3))
+            def _():
+                then(2 * i + table.core, 2 * i + 1 - table.core)
+
+    def absorb_pair(own, other):
+        absorb(own, 0, 4)
+        for piece in range(CHUNKS):
+            table.wait(other, piece)
+        absorb(other, 0, 4)
+
+    u_copy.wait()
+    absorb_pair(place.s, place.s + 1 - 2 * table.core)
+    each_side(1, absorb_pair)
+    table.relay(2, 3)
+    each_side(2, absorb_pair)
+
+    @pl.loop(0, 16)
+    def _(p):
+        for zh in (0, 1):
+            xt[p, zh] = xbuf[p, zh].astype(F32).T.astype(BF16)
+
+    x_copy = pltpu.make_async_copy(xt, x_out, x_sem)
+    x_copy.start()
     for piece in range(CHUNKS):
-        table.wait(other, piece)
-    absorb(other, 0, 4)
-    for wave in (1, 2, 3):
-        if wave == 3:
-
-            @pl.loop(0, 16)
-            def _(p):
-                for zh in (0, 1):
-                    xt[p, zh] = xbuf[p, zh].astype(F32).T.astype(BF16)
-
-            x_copy = pltpu.make_async_copy(xt, x_out, x_sem)
-            x_copy.start()
-        for piece in range(CHUNKS):
-            if wave == 3:
-                table.relay(3, piece)
-            for side in (-1, 1):
-                i = table.zl + side * wave
-
-                @pl.when((i >= 0) & (i <= 3))
-                def _():
-                    per = 4 // CHUNKS
-                    absorb(2 * i + table.core, piece * per, per)
-                    table.wait(2 * i + 1 - table.core, piece)
-                    absorb(2 * i + 1 - table.core, piece * per, per)
-
+        table.relay(3, piece)
+
+        def absorb_piece(own, other):
+            absorb(own, piece, 1)
+            table.wait(other, piece)
+            absorb(other, piece, 1)
+
+        each_side(3, absorb_piece)
     wait_stats(place, scale_stats, sts1, str1)
     scale = lax.rsqrt(jnp.sum(scale_stats[...], axis=0) / D + EPS)
 
@@ -490,111 +595,35 @@
     l_norm, t_norm, pull = columns[:, 0:1], columns[:, 1:2], columns[:, 2:3]
     dlogits = (jnp.exp(logits - l_norm) - jnp.exp(target - t_norm)).astype(BF16)
 
-    ids = {}
-    sent = []
-    half_rows, quarter = ROWS // 2, ROWS // 4
-
-    def span(half, name):
-        if name == "all":
-            return pl.ds(half * half_rows, half_rows)
-        return pl.ds(half * half_rows + (0 if name == "first" else quarter), quarter)
-
-    def product(pair):
+    def product(pair, level):
         y, x = pair // 4, lax.rem(pair, 4)
-        for zh in (0, 1):
-            rows = pl.ds(pl.multiple_of(x * FB, FB), FB)
-            part[pair, zh] = lax.dot_general(
-                dlogits, u[2 * y + zh, rows, :], (((1,), (1,)), ((), ())), preferred_element_type=F32
-            )
-
-    def move(name, src, dst, device):
-        k = ids.setdefault(name, len(ids))
-        return remote(src, dst, ss.at[k], rs.at[k], device)
-
-    def landing(stage, name, step, pair, half):
-        rows = span(half, name)
-        if name != "all":
-            return rq.at[pair, :, rows, :]
-        if stage == 2:
-            return (rp if step == 1 else rm).at[pair, :, rows, :]
-        return (r1p if step == 1 else r1m).at[:, rows, :]
-
-    def send(half, stage, col, c, d, name, step):
-        pair = place.pair(half, c, d)
-        copy = move(
-            (half, stage, col, name, step),
-            sbuf.at[pair, :, span(half, name), :],
-            landing(stage, name, step, pair, half),
-            place.near(half, stage, step),
+        rows = pl.ds(pl.multiple_of(x * FB, FB), FB)
+        part[pair, level] = lax.dot_general(
+            dlogits, u[2 * y + level, rows, :], (((1,), (1,)), ((), ())), preferred_element_type=F32
         )
-        copy.start()
-        sent.append(copy)
-
-    def receive(half, stage, col, c, d, name, step):
-        pair = place.pair(half, c, d)
-        ref = landing(stage, name, step, pair, half)
-        move((half, stage, col, name, step), ref, ref, place.near(half, stage, -step)).wait_recv()
-        return ref[...].astype(F32)
-
-    def put(half, c, d, name, value):
-        sbuf[place.pair(half, c, d), :, span(half, name), :] = value.astype(BF16)
-
-    def mine(half, c, d, name):
-        return part[place.pair(half, c, d), :, span(half, name), :]
-
-    first = [(2, 2)] + [(2, k) for k in (-1, 1, 0)] + [(k, 2) for k in (-1, 1, 0)]
-    later = [(-1, -1), (-1, 1), (1, -1), (1, 1), (0, -1), (0, 1), (-1, 0), (1, 0), (0, 0)]
-    for dx, dy in first:
-        product(place.pair(0, dx, dy))
-        for half in (0, 1):
-            c, d = (dx, dy) if half == 0 else (dy, dx)
-            if d == 2:
-                put(half, c, 2, "all", mine(half, c, 2, "all"))
-                send(half, 2, c, c, 2, "first", -1)
-                send(half, 2, c, c, 2, "second", 1)
-    for dx, dy in later:
-        product(place.pair(0, dx, dy))
-    order = (2, -1, 1, 0)
-    for c in order:
-        for half in (0, 1):
-            for step, name in ((-1, "first"), (1, "second")):
-                arrived = receive(half, 2, c, c, step, name, step)
-                put(half, c, step, "all", mine(half, c, step, "all"))
-                put(half, c, step, name, mine(half, c, step, name) + arrived)
-                send(half, 2, c, c, step, "all", step)
-    own_sum = [None, None]
-    for c in order:
-        for half in (0, 1):
-            total = mine(half, c, 0, "all")
-            for step in (1, -1):
-                total = total + receive(half, 2, c, c, 0, "all", step)
-            if c == 2:
-                put(half, 2, 0, "all", total)
-                send(half, 1, 0, 2, 0, "first", -1)
-                send(half, 1, 0, 2, 0, "second", 1)
-            elif c != 0:
-                name = "first" if c == -1 else "second"
-                arrived = receive(half, 1, 0, c, 0, name, c)
-                zero = jnp.zeros_like(arrived)
-                pieces = [arrived, zero] if name == "first" else [zero, arrived]
-                put(half, c, 0, "all", total + jnp.concatenate(pieces, axis=1))
-                send(half, 1, 0, c, 0, "all", c)
-            else:
-                for step in (1, -1):
-                    total = total + receive(half, 1, 0, 0, 0, "all", step)
-                put(half, 0, 0, "all", total)
-                part[place.own, :, span(half, "all"), :] = total
-    out = remote(sbuf.at[place.own, 1 - place.zh], rz, zs.at[2], zr.at[2], place.partner())
+
+    refs = (part, sbuf, (rq, rp, rm), (r1p, r1m, r1q))
+    far = Scatter(place, 1 - place.zh, product, refs, ss.at[0], rs.at[0])
+    near = Scatter(place, place.zh, product, refs, ss.at[1], rs.at[1])
+    far.open()
+    near.open()
+    far.turn()
+    near.turn()
+    far.close()
+    out = remote(sbuf.at[place.own, 1 - place.zh], rz, zs.at[3], zr.at[3], place.partner())
     out.start()
+    near.close()
     out.wait_recv()
     dnormed = part[place.own, place.zh] + rz[...].astype(F32)
     scaled = dnormed * gain_cols
     dtrans_out[...] = trans_scale * (scaled - trans_ref[...] * pull)
     out.wait_send()
-    for copy in sent:
+    for copy in far.sent + near.sent:
         copy.wait_send()
-    gather_x.drain()
-    gather_lt.drain()
+    for copy in (cross_x, cross_t, cross_l):
+        copy.wait_send()
+    for steps in planes:
+        steps.drain()
     table.drain()
     pool.drain()
     x_copy.wait()
@@ -646,6 +675,7 @@
             block,
             pltpu.VMEM((2, ROWS, FB), BF16),
             pltpu.VMEM((2, ROWS, FB), BF16),
+            pltpu.VMEM((2, ROWS, FB), BF16),
             pltpu.VMEM((ROWS, FB), BF16),
             dma((3,)),
             dma,
@@ -656,11 +686,13 @@
             dma((4,)),
             dma((4,)),
             dma((NS,)),
-            pltpu.SemaphoreType.REGULAR((3, 2)),
-            dma((3,)),
-            dma((3,)),
+            pltpu.SemaphoreType.REGULAR((5, 2)),
+            dma((4,)),
+            dma((4,)),
+            dma((6, N_MSG)),
+            dma((6, N_MSG)),
         ]
-        + [dma((N_MSG,))] * 6
+        + [dma((2, N_MSG))] * 2
         + [dma((NV,))] * 4,
         compiler_params=pltpu.CompilerParams(
             collective_id=0, has_side_effects=True, vmem_limit_bytes=VMEM_LIMIT

time: 144 us -> 135 us (0.938)
  Pallas kernels: 143 us -> 133 us
    pallas_call x1, Pallas kernels: 138 us -> 128 us  [per_device(): pl.pallas_call(kernel, name='lens', out_shape=(shape((16, 2, FB, ROWS), B...]
where the time goes in v4:
time: 135 us; the launch traced here: 134 us
  Pallas kernels  133 us (99%)
    pallas_call x1, Pallas kernels, per_device(): pl.pallas_call(kernel, name='lens', out_shape=(shape((16, 2, FB, ROWS), B...  128 us
    pallas_call x1, Pallas kernels, per_device(): pl.pallas_call(last_kernel, name='weight_gradient', grid=(4,), out_shape=...  5.04 us

profile of v4, /device:TPU:2, one launch (start us, length us, event | category | flops | bytes accessed | tf_op | source)
XLA Modules:
  0.0 133.5 jit_solution(3554630968009058003)
XLA Ops:
  0.6 127.7 %lens.1 = (bf16[16,2,256,128]{3,2,1,0:T(8,128)(2,1)}, f32[128,256]{1,0:T(8,128)}, f32[1,128]{1,0:T(1,128)}) custom-call(s32[1,128]{1,0:T(1,128)} %pick.1, bf16[512,256]{1,0:T(8,128)(2,1)} %bitcast.4, bf16[64,256]{1,0:T(8,128)(2,1)} %final_hbm.1, bf16[8192,256]{1,0:T(8,128)(2,1)} %bitcast.3, bf16[1,256]{1,0:T(2,128)(2,1)} %bias.1, bf16[256]{0:T(256)(128)(2,1)} %gain.1, ...), custom_call_target="tpu_custom_call" | custom-call | tf_op jit(solution)/shard_map/lens/pallas_call | solution.py:653
  128.3 5.0 %weight_gradient.1 = (bf16[8192,256]{1,0:T(8,128)(2,1)}, f32[1,256]{1,0:T(1,128)}, f32[1]{0:T(128)}) custom-call(bf16[16,2,256,128]{3,2,1,0:T(8,128)(2,1)} %get-tuple-element.9.x, f32[128,256]{1,0:T(8,128)} %get-tuple-element.10.dtrans, f32[1,128]{1,0:T(1,128)} %get-tuple-element.11.kl), custom_call_target="tpu_custom_call" | custom-call | tf_op jit(solution)/shard_map/weight_gradient/pallas_call | solution.py:701

commit v5 on v4

--- a/solution.py
+++ b/solution.py
@@ -606,12 +606,12 @@
     far = Scatter(place, 1 - place.zh, product, refs, ss.at[0], rs.at[0])
     near = Scatter(place, place.zh, product, refs, ss.at[1], rs.at[1])
     far.open()
+    far.turn()
     near.open()
-    far.turn()
-    near.turn()
     far.close()
     out = remote(sbuf.at[place.own, 1 - place.zh], rz, zs.at[3], zr.at[3], place.partner())
     out.start()
+    near.turn()
     near.close()
     out.wait_recv()
     dnormed = part[place.own, place.zh] + rz[...].astype(F32)
@@ -631,9 +631,9 @@
 
 def last_kernel(x, dtrans, kl, grad, grad_bias, kl_mean):
     rounded = dtrans[...].astype(BF16)
-    for k in range(4):
+    for k in range(8):
         for zh in (0, 1):
-            v = zh * 4 + k
+            v = (k // 4) * 8 + zh * 4 + k % 4
             grad[v * FB : (v + 1) * FB, :] = lax.dot_general(
                 x[k, zh], rounded, (((1,), (0,)), ((), ())), preferred_element_type=F32
             ).astype(BF16)
@@ -701,15 +701,15 @@
     grad_weight, grad_bias, kl_mean = pl.pallas_call(
         last_kernel,
         name="weight_gradient",
-        grid=(4,),
+        grid=(2,),
         out_shape=(shape((D, FB), BF16), shape((1, FB), F32), shape((1,), F32)),
         in_specs=[
-            pl.BlockSpec((4, 2, FB, ROWS), lambda y: (y, 0, 0, 0)),
+            pl.BlockSpec((8, 2, FB, ROWS), lambda y: (y, 0, 0, 0)),
             pl.BlockSpec((ROWS, FB), lambda y: (0, 0)),
             pl.BlockSpec((1, ROWS), lambda y: (0, 0)),
         ],
         out_specs=(
-            pl.BlockSpec((D // 4, FB), lambda y: (y, 0)),
+            pl.BlockSpec((D // 2, FB), lambda y: (y, 0)),
             pl.BlockSpec((1, FB), lambda y: (0, 0)),
             pl.BlockSpec(memory_space=pltpu.SMEM),
         ),

time: 135 us -> 133 us (0.985)
  Pallas kernels: 133 us -> 131 us
where the time goes in v5:
time: 133 us; the launch traced here: 132 us
  Pallas kernels  131 us (98%)
    pallas_call x1, Pallas kernels, per_device(): pl.pallas_call(kernel, name='lens', out_shape=(shape((16, 2, FB, ROWS), B...  127 us
    pallas_call x1, Pallas kernels, per_device(): pl.pallas_call(last_kernel, name='weight_gradient', grid=(2,), out_shape=...  4.09 us

profile of v5, /device:TPU:2, one launch (start us, length us, event | category | flops | bytes accessed | tf_op | source)
XLA Modules:
  0.0 132.1 jit_solution(9909229255882858846)
XLA Ops:
  0.6 127.3 %lens.1 = (bf16[16,2,256,128]{3,2,1,0:T(8,128)(2,1)}, f32[128,256]{1,0:T(8,128)}, f32[1,128]{1,0:T(1,128)}) custom-call(s32[1,128]{1,0:T(1,128)} %pick.1, bf16[512,256]{1,0:T(8,128)(2,1)} %bitcast.4, bf16[64,256]{1,0:T(8,128)(2,1)} %final_hbm.1, bf16[8192,256]{1,0:T(8,128)(2,1)} %bitcast.3, bf16[1,256]{1,0:T(2,128)(2,1)} %bias.1, bf16[256]{0:T(256)(128)(2,1)} %gain.1, ...), custom_call_target="tpu_custom_call" | custom-call | tf_op jit(solution)/shard_map/lens/pallas_call | solution.py:653
  127.9 4.1 %weight_gradient.1 = (bf16[8192,256]{1,0:T(8,128)(2,1)}, f32[1,256]{1,0:T(1,128)}, f32[1]{0:T(128)}) custom-call(bf16[16,2,256,128]{3,2,1,0:T(8,128)(2,1)} %get-tuple-element.9.x, f32[128,256]{1,0:T(8,128)} %get-tuple-element.10.dtrans, f32[1,128]{1,0:T(1,128)} %get-tuple-element.11.kl), custom_call_target="tpu_custom_call" | custom-call | tf_op jit(solution)/shard_map/weight_gradient/pallas_call | solution.py:701
